TPU v7x, 1024 devices: a whole 4x4x32 slice. The times are simulated.
1024 devices in a mesh: grp: 4 (over y_lo, core), lat: 32 (over z), lon: 8 (over x, y_hi).
Axes of the slice: x: 4, y: 4 (y_hi: 2, y_lo: 2; y = y_hi * 2 + y_lo), z: 32, core: 2. Of those that a mesh axis runs over, the one named last changes fastest.
Arguments:
- grid_state: bfloat16 [32, 2560, 5120], P(None, ('grp', 'lat'), 'lon'), may hold values from -6 to 6
- legendre: bfloat16 [128, 1920, 1280], P(('grp', 'lat')), may hold values from -0.125 to 0.125
- sent_field: float32 [2560, 5120], P(('grp', 'lat'), 'lon'), may hold values from -6 to 6
- wet_mask: int32 [2560, 5120], P(('grp', 'lat'), 'lon'), may hold values from 0 to 1, as said below
- diffusivity: float32 [2560, 5120], P(('grp', 'lat'), 'lon'), may hold values from 0.04 to 0.24
- remap_blocks: int32 [128, 8, 8, 3], P(('grp', 'lat'), 'lon'), may hold values from 0 to 99, as said below
- remap_weights: bfloat16 [128, 8, 8, 128, 128], P(('grp', 'lat'), 'lon'), may hold values from -0.5 to 0.5
Outputs:
- spectral: float32 [128, 32, 2, 1280], P(('grp', 'lat'), 'lon')
- received: float32 [2560, 5120], P(('grp', 'lat'), 'lon')
- grid_next: float32 [32, 2560, 5120], P(None, ('grp', 'lat'), 'lon')
Inputs may be any that keep to these rules, and one draw needn't show every extreme that they name: wet_mask is 1 on every row below 1920. remap_blocks: field 0 is 3 h + d + 1 with d in -1..1 and h the source group: h = 3 on atmosphere bands, h below 3 on ocean bands; fields 1 and 2 are below 100; entry 0 of every tile names source block 0 and target block 99.
All inputs are finite; a program needn't handle non-finite values.
Results may differ from a plain program's by a relative error of at most 0.0037.
Values may be sent and summed in bfloat16 or wider, within the bound.
No kernel may reach another device: no remote copies, remote signals or barrier semaphores. Data moves between devices by JAX's collectives and lax.ppermute only.
A program may use at most 32 MiB of HBM per device.

v0:
```python
import math

import jax
import jax.numpy as jnp
from jax import lax
from jax.sharding import PartitionSpec as P


def with_halo(cells, sides, width):
    for axis, dim in sides:
        count = lax.axis_size(axis)
        head = lax.slice_in_dim(cells, 0, width, axis=dim)
        tail = lax.slice_in_dim(cells, cells.shape[dim] - width, cells.shape[dim], axis=dim)
        cells = jnp.concatenate(
            [
                lax.ppermute(tail, axis, [(i, (i + 1) % count) for i in range(count)]),
                cells,
                lax.ppermute(head, axis, [((i + 1) % count, i) for i in range(count)]),
            ],
            axis=dim,
        )
    return cells


def fourier_table(wave_count, lon_first, lon_count, lon_total):
    wave_ids = jnp.arange(wave_count, dtype=jnp.int32)
    longitudes = lon_first + jnp.arange(lon_count, dtype=jnp.int32)
    phases = wave_ids[:, None] * longitudes[None, :] % lon_total
    angles = jnp.float32(2.0 * math.pi / lon_total) * phases.astype(jnp.float32)
    basis_rows = jnp.stack([jnp.cos(angles), -jnp.sin(angles)], axis=1)
    return basis_rows.reshape(2 * wave_count, lon_count).astype(jnp.bfloat16)


def relax(padded_state, padded_wet, diffusion):
    height = padded_state.shape[1] - 2
    breadth = padded_state.shape[2] - 2
    centre = padded_state[:, 1:-1, 1:-1]
    centre_wet = padded_wet[1:-1, 1:-1]
    laplace_sum = jnp.zeros_like(centre)
    for row_shift, col_shift in ((0, 1), (0, -1), (1, 0), (-1, 0)):
        neighbour = padded_state[
            :, 1 + row_shift : 1 + row_shift + height, 1 + col_shift : 1 + col_shift + breadth
        ]
        neighbour_wet = padded_wet[
            1 + row_shift : 1 + row_shift + height, 1 + col_shift : 1 + col_shift + breadth
        ]
        laplace_sum = laplace_sum + neighbour_wet * (neighbour - centre)
    return centre + diffusion * centre_wet * laplace_sum


def shards(grid_state, legendre, sent_field, wet_mask, diffusivity, remap_blocks, remap_weights):
    lon_tiles = lax.axis_size("lon")
    band_count = lax.axis_size(("grp", "lat"))
    lon_local = grid_state.shape[2]
    lon_total = lon_local * lon_tiles
    wave_count = band_count * legendre.shape[0]
    norm_factor = jnp.float32(1.0 / math.sqrt(lon_total))
    local_basis = fourier_table(wave_count, lax.axis_index("lon") * lon_local, lon_local, lon_total)
    summed = lax.psum_scatter(
        jnp.einsum("fal,cl->fca", grid_state, local_basis, preferred_element_type=jnp.float32)
        * norm_factor,
        "lon",
        scatter_dimension=0,
        tiled=True,
    )
    fourier = summed.astype(jnp.bfloat16)
    wave_rows = lax.all_to_all(fourier, ("grp", "lat"), split_axis=1, concat_axis=2, tiled=True)
    lat_total = legendre.shape[1]
    wave_rows = wave_rows[:, :, :lat_total]
    wave_rows = wave_rows.reshape(wave_rows.shape[0], legendre.shape[0], 2, lat_total)
    spectral = jnp.einsum("fmpl,mln->mfpn", wave_rows, legendre, preferred_element_type=jnp.float32)
    block_cells = remap_weights.shape[-1]
    own_blocks = sent_field.astype(jnp.bfloat16).reshape(1, -1, block_cells)
    tile_blocks = own_blocks.shape[1]
    lon_near = with_halo(own_blocks, (("lon", 0),), 1)
    near_tiles = lax.all_gather(lon_near, "grp", axis=0, tiled=True)
    near_tiles = near_tiles.reshape(-1, block_cells)
    listing = remap_blocks[0, 0]
    rows_at = listing[:, 0] * tile_blocks + listing[:, 1]
    sources = jnp.take(near_tiles, rows_at, axis=0)
    products = jnp.einsum(
        "eij,ej->ei", remap_weights[0, 0], sources, preferred_element_type=jnp.float32
    )
    onehot = (listing[:, 2][None, :] == jnp.arange(tile_blocks, dtype=jnp.int32)[:, None]).astype(
        jnp.float32
    )
    received = jnp.dot(onehot, products, precision=lax.Precision.HIGHEST).reshape(sent_field.shape)
    wet_field = wet_mask.astype(jnp.float32)
    forced = grid_state.astype(jnp.float32).at[0].add(wet_field * received)
    grid_next = forced
    for repeat in range(2):
        stacked = jnp.concatenate([grid_next, wet_field[None]], axis=0)
        padded = with_halo(stacked, ((("grp", "lat"), 1), ("lon", 2)), 1)
        grid_next = relax(padded[:-1], padded[-1], diffusivity)
    return (spectral, received, grid_next)


def solution(mesh):
    in_specs = (
        P(None, ("grp", "lat"), "lon"),
        P(("grp", "lat"), None, None),
        P(("grp", "lat"), "lon"),
        P(("grp", "lat"), "lon"),
        P(("grp", "lat"), "lon"),
        P(("grp", "lat"), "lon", None, None),
        P(("grp", "lat"), "lon", None, None, None),
    )
    out_specs = (
        P(("grp", "lat"), "lon", None, None),
        P(("grp", "lat"), "lon"),
        P(None, ("grp", "lat"), "lon"),
    )
    return jax.shard_map(shards, mesh=mesh, in_specs=in_specs, out_specs=out_specs, check_vma=False)
```

profile of v0, /device:TPU:1, one launch (start us, length us, event | category | flops | bytes accessed | tf_op | source)
XLA Modules:
  0.0 214.7 jit_solution(212498672812562382)
XLA Ops:
  0.7 0.9 convert_element_type.34
  1.6 5.6 %collective-permute-start = (bf16[1,100,128]{2,1,0:T(8,128)(2,1)S(1)}, bf16[1,100,128]{2,1,0:T(8,128)(2,1)S(1)}, u32[]{:S(2)}, u32[]{:S(2)}) collective-permute-start(bf16[1,100,128]{2,1,0:T(8,128)(2,1)S(1)} %reshape.158), channel_id=1, source_target_pairs={{0,1},{1,2},{2,3},{3,4},{4,5},{5,6},{6,7},{7,0},{8,9},{9,10},{10,1... | collective-permute-start | bytes 76808 | tf_op jit(solution)/shard_map/ppermute | solution.py:16
  7.2 4.1 %collective-permute-start.1 = (bf16[1,100,128]{2,1,0:T(8,128)(2,1)S(1)}, bf16[1,100,128]{2,1,0:T(8,128)(2,1)S(1)}, u32[]{:S(2)}, u32[]{:S(2)}) collective-permute-start(bf16[1,100,128]{2,1,0:T(8,128)(2,1)S(1)} %reshape.158), channel_id=1, source_target_pairs={{1,0},{2,1},{3,2},{4,3},{5,4},{6,5},{7,6},{0,7},{9,8},{10,9},{11,1... | collective-permute-start | bytes 76808 | tf_op jit(solution)/shard_map/ppermute | solution.py:18
  11.4 0.7 copy.62
  12.1 1.4 copy_convert_fusion
  13.5 1.4 cosine_convert_fusion
  15.0 19.6 %all_gather.3 = bf16[12,100,128]{2,1,0:T(8,128)(2,1)S(1)} all-gather(bf16[3,100,128]{2,1,0:T(8,128)(2,1)S(1)} %pad_maximum_fusion.13), channel_id=1, replica_groups=mesh['grp'=4,'lat'=32,'lon'=8] {'grp'}, dimensions={0}, use_global_device_ids=true | all-gather | bytes 384000 | tf_op jit(solution)/shard_map/all_gather | solution.py:76
  35.8 0.8 pad_maximum_fusion.12
  36.6 1.9 collective-permute-start.2
  38.5 6.0 %collective-permute-start.3 = (f32[33,1,640]{2,1,0:T(1,128)S(1)}, f32[33,1,640]{2,1,0:T(1,128)S(1)}, u32[]{:S(2)}, u32[]{:S(2)}) collective-permute-start(f32[33,1,640]{2,1,0:T(1,128)S(1)} %get-tuple-element.41), channel_id=1, source_target_pairs={{8,0},{16,8},{24,16},{32,24},{40,32},{48,40},{56,48},{64,56},{72,6... | collective-permute-start | bytes 253448 | tf_op jit(solution)/shard_map/ppermute | solution.py:18
  45.1 0.7 collective-permute-done.2
  46.5 3.6 %collective-permute-start.4 = (f32[33,22,1]{2,1,0:T(8,128)S(1)}, f32[33,22,1]{2,1,0:T(8,128)S(1)}, u32[]{:S(2)}, u32[]{:S(2)}) collective-permute-start(f32[33,22,1]{2,1,0:T(8,128)S(1)} %get-tuple-element.40), channel_id=1, source_target_pairs={{0,1},{1,2},{2,3},{3,4},{4,5},{5,6},{6,7},{7,0},{8,9},{9,10},{10,1... | collective-permute-start | bytes 8720 | tf_op jit(solution)/shard_map/ppermute | solution.py:16
  50.2 5.3 %collective-permute-start.5 = (f32[33,22,1]{2,1,0:T(8,128)S(1)}, f32[33,22,1]{2,1,0:T(8,128)S(1)}, u32[]{:S(2)}, u32[]{:S(2)}) collective-permute-start(f32[33,22,1]{2,1,0:T(8,128)S(1)} %get-tuple-element.39), channel_id=1, source_target_pairs={{1,0},{2,1},{3,2},{4,3},{5,4},{6,5},{7,6},{0,7},{9,8},{10,9},{11,1... | collective-permute-start | bytes 8720 | tf_op jit(solution)/shard_map/ppermute | solution.py:18
  55.9 9.9 %collective-permute-done.4 = f32[33,22,1]{2,1,0:T(8,128)S(1)} collective-permute-done((f32[33,22,1]{2,1,0:T(8,128)S(1)}, f32[33,22,1]{2,1,0:T(8,128)S(1)}, u32[]{:S(2)}, u32[]{:S(2)}) %collective-permute-start.4) | collective-permute-done | bytes 2936 | tf_op jit(solution)/shard_map/ppermute | solution.py:16
  65.8 6.2 %collective-permute-done.5 = f32[33,22,1]{2,1,0:T(8,128)S(1)} collective-permute-done((f32[33,22,1]{2,1,0:T(8,128)S(1)}, f32[33,22,1]{2,1,0:T(8,128)S(1)}, u32[]{:S(2)}, u32[]{:S(2)}) %collective-permute-start.5) | collective-permute-done | bytes 2936 | tf_op jit(solution)/shard_map/ppermute | solution.py:18
  72.3 6.3 %fusion.18 = f32[32,20,640]{2,1,0:T(8,128)S(1)} fusion(f32[32,20,640]{2,1,0:T(8,128)S(1)} %fusion.71, f32[1,20,640]{2,1,0:T(8,128)S(1)} %convert_bitcast_fusion, f32[33,1,640]{2,1,0:T(1,128)S(1)} %collective-permute-done.2, f32[33,1,640]{2,1,0:T(1,128)S(1)} %collective-permute-done.3, f32[33,22,1]{2,1,0:T(8,128)S(1)} %collective-permute-done.4, ...), kind=kLoop, calls=%fused_computation.30 | loop fusion | flops 10240000 | bytes 3758768 | tf_op jit(solution)/shard_map/add | solution.py:48
  78.6 1.3 copy-done.1
  80.0 1.9 collective-permute-start.6
  81.9 6.4 %collective-permute-start.7 = (f32[33,1,640]{2,1,0:T(1,128)S(1)}, f32[33,1,640]{2,1,0:T(1,128)S(1)}, u32[]{:S(2)}, u32[]{:S(2)}) collective-permute-start(f32[33,1,640]{2,1,0:T(1,128)S(1)} %get-tuple-element.37), channel_id=1, source_target_pairs={{8,0},{16,8},{24,16},{32,24},{40,32},{48,40},{56,48},{64,56},{72,6... | collective-permute-start | bytes 253448 | tf_op jit(solution)/shard_map/ppermute | solution.py:18
  88.4 38.2 %all-reduce.2 = bf16[32,256,20]{1,0,2:T(8,128)(2,1)} all-reduce(f32[32,256,20]{1,0,2:T(8,128)S(1)} %fusion.51), channel_id=2, replica_groups=mesh['grp'=4,'lat'=32,'lon'=8] {'lon'}, use_global_device_ids=true, to_apply=%region_0.1.clone | all-reduce | flops 163840 | bytes 983040
  126.6 1.3 dynamic-slice.8
  128.5 1.9 fusion.8
  130.4 1.0 fusion.76
  131.4 3.3 %collective-permute-start.8 = (f32[33,22,1]{2,1,0:T(8,128)}, f32[33,22,1]{2,1,0:T(8,128)S(1)}, u32[]{:S(2)}, u32[]{:S(2)}) collective-permute-start(f32[33,22,1]{2,1,0:T(8,128)} %get-tuple-element.36), channel_id=1, source_target_pairs={{0,1},{1,2},{2,3},{3,4},{4,5},{5,6},{6,7},{7,0},{8,9},{9,10},{10,1... | collective-permute-start | bytes 8720 | tf_op jit(solution)/shard_map/ppermute | solution.py:16
  134.7 5.6 %collective-permute-start.9 = (f32[33,22,1]{2,1,0:T(8,128)}, f32[33,22,1]{2,1,0:T(8,128)S(1)}, u32[]{:S(2)}, u32[]{:S(2)}) collective-permute-start(f32[33,22,1]{2,1,0:T(8,128)} %get-tuple-element.35), channel_id=1, source_target_pairs={{1,0},{2,1},{3,2},{4,3},{5,4},{6,5},{7,6},{0,7},{9,8},{10,9},{11,1... | collective-permute-start | bytes 8720 | tf_op jit(solution)/shard_map/ppermute | solution.py:18
  140.3 0.9 dynamic-slice_convert_fusion
  141.2 0.9 copy.44
  142.1 24.9 %all-to-all-start = ((bf16[4,256,20]{2,0,1:T(4,128)(2,1)}), bf16[4,256,20]{2,0,1:T(4,128)(2,1)S(1)}, u32[]{:S(2)}, u32[]{:S(2)}) async-start(bf16[4,256,20]{2,0,1:T(4,128)(2,1)} %copy.44), calls=%async_computation | async-start | bytes 524288 | tf_op jit(solution)/shard_map/all_to_all | solution.py:67
  168.0 6.3 %fusion.28 = f32[32,20,640]{2,1,0:T(8,128)S(1)} fusion(f32[32,20,640]{2,1,0:T(8,128)S(1)} %copy-done.2, f32[1,20,640]{2,1,0:T(8,128)S(1)} %convert_bitcast_fusion, f32[33,1,640]{2,1,0:T(1,128)S(1)} %collective-permute-done.6, f32[33,1,640]{2,1,0:T(1,128)S(1)} %collective-permute-done.7, f32[33,22,1]{2,1,0:T(8,128)S(1)} %collective-permute-done.8, ...), kind=kLoop, calls=%fused_computation.40 | loop fusion | flops 10240000 | bytes 3758768 | tf_op jit(solution)/shard_map/add | solution.py:48
  174.2 1.5 copy.50
  175.7 34.6 %all-to-all-done = bf16[4,256,20]{2,0,1:T(4,128)(2,1)S(1)} async-done(((bf16[4,256,20]{2,0,1:T(4,128)(2,1)}), bf16[4,256,20]{2,0,1:T(4,128)(2,1)S(1)}, u32[]{:S(2)}, u32[]{:S(2)}) %all-to-all-start) | async-done | bytes 40992 | tf_op jit(solution)/shard_map/all_to_all | solution.py:67
  210.8 3.2 %fusion.2 = f32[1,4,2,1280]{3,1,2,0:T(4,128)S(1)} fusion(bf16[1,1920,1280]{2,1,0:T(8,128)(2,1)} %param.10, bf16[4,2,2560]{2,0,1:T(4,128)(2,1)S(1)} %reshape.175), kind=kOutput, calls=%fused_computation.13 | convolution fusion | flops 39321600 | bytes 4986880 | tf_op jit(solution)/shard_map/fmpl,mln->mfpn/dot_general | solution.py:71
  (51 shorter events, 5.3 us)
Async XLA Ops:
  0.6 34.7 %copy-start = (bf16[1,1,8,128,128]{4,3,2,1,0:T(8,128)(2,1)S(1)}, bf16[1,1,8,128,128]{4,3,2,1,0:T(8,128)(2,1)}, u32[]{:S(2)}) copy-start(bf16[1,1,8,128,128]{4,3,2,1,0:T(8,128)(2,1)} %param.15) | copy-start | bytes 786436
  0.6 12.9 %copy-start.5 = (s32[20,640]{1,0:T(8,128)S(1)}, s32[20,640]{1,0:T(8,128)}, u32[]{:S(2)}) copy-start(s32[20,640]{1,0:T(8,128)} %param.12) | copy-start | bytes 153604
  1.6 13.4 %collective-permute-start = (bf16[1,100,128]{2,1,0:T(8,128)(2,1)S(1)}, bf16[1,100,128]{2,1,0:T(8,128)(2,1)S(1)}, u32[]{:S(2)}, u32[]{:S(2)}) collective-permute-start(bf16[1,100,128]{2,1,0:T(8,128)(2,1)S(1)} %reshape.158), channel_id=1, source_target_pairs={{0,1},{1,2},{2,3},{3,4},{4,5},{5,6},{6,7},{7,0},{8,9},{9,10},{10,1... | collective-permute-start | bytes 76808 | tf_op jit(solution)/shard_map/ppermute | solution.py:16
  7.2 7.8 %collective-permute-start.1 = (bf16[1,100,128]{2,1,0:T(8,128)(2,1)S(1)}, bf16[1,100,128]{2,1,0:T(8,128)(2,1)S(1)}, u32[]{:S(2)}, u32[]{:S(2)}) collective-permute-start(bf16[1,100,128]{2,1,0:T(8,128)(2,1)S(1)} %reshape.158), channel_id=1, source_target_pairs={{1,0},{2,1},{3,2},{4,3},{5,4},{6,5},{7,6},{0,7},{9,8},{10,9},{11,1... | collective-permute-start | bytes 76808 | tf_op jit(solution)/shard_map/ppermute | solution.py:18
  35.8 8.8 %copy-start.4 = (f32[20,640]{1,0:T(8,128)}, f32[20,640]{1,0:T(8,128)S(1)}, u32[]{:S(2)}) copy-start(f32[20,640]{1,0:T(8,128)S(1)} %reshape.160) | copy-start | bytes 153604
  36.6 9.2 %collective-permute-start.2 = (f32[33,1,640]{2,1,0:T(1,128)}, f32[33,1,640]{2,1,0:T(1,128)S(1)}, u32[]{:S(2)}, u32[]{:S(2)}) collective-permute-start(f32[33,1,640]{2,1,0:T(1,128)} %get-tuple-element.42), channel_id=1, source_target_pairs={{0,8},{8,16},{16,24},{24,32},{32,40},{40,48},{48,56},{56,64},{64,7... | collective-permute-start | bytes 253448 | tf_op jit(solution)/shard_map/ppermute | solution.py:16
  38.5 7.5 %collective-permute-start.3 = (f32[33,1,640]{2,1,0:T(1,128)S(1)}, f32[33,1,640]{2,1,0:T(1,128)S(1)}, u32[]{:S(2)}, u32[]{:S(2)}) collective-permute-start(f32[33,1,640]{2,1,0:T(1,128)S(1)} %get-tuple-element.41), channel_id=1, source_target_pairs={{8,0},{16,8},{24,16},{32,24},{40,32},{48,40},{56,48},{64,56},{72,6... | collective-permute-start | bytes 253448 | tf_op jit(solution)/shard_map/ppermute | solution.py:18
  45.1 10.4 %copy-start.3 = (bf16[32,20,640]{2,0,1:T(8,128)(2,1)S(1)}, bf16[32,20,640]{2,0,1:T(8,128)(2,1)}, u32[]{:S(2)}) copy-start(bf16[32,20,640]{2,0,1:T(8,128)(2,1)} %param.9) | copy-start | bytes 2457604
  46.5 19.3 %collective-permute-start.4 = (f32[33,22,1]{2,1,0:T(8,128)S(1)}, f32[33,22,1]{2,1,0:T(8,128)S(1)}, u32[]{:S(2)}, u32[]{:S(2)}) collective-permute-start(f32[33,22,1]{2,1,0:T(8,128)S(1)} %get-tuple-element.40), channel_id=1, source_target_pairs={{0,1},{1,2},{2,3},{3,4},{4,5},{5,6},{6,7},{7,0},{8,9},{9,10},{10,1... | collective-permute-start | bytes 8720 | tf_op jit(solution)/shard_map/ppermute | solution.py:16
  50.2 21.9 %collective-permute-start.5 = (f32[33,22,1]{2,1,0:T(8,128)S(1)}, f32[33,22,1]{2,1,0:T(8,128)S(1)}, u32[]{:S(2)}, u32[]{:S(2)}) collective-permute-start(f32[33,22,1]{2,1,0:T(8,128)S(1)} %get-tuple-element.39), channel_id=1, source_target_pairs={{1,0},{2,1},{3,2},{4,3},{5,4},{6,5},{7,6},{0,7},{9,8},{10,9},{11,1... | collective-permute-start | bytes 8720 | tf_op jit(solution)/shard_map/ppermute | solution.py:18
  55.9 16.2 %copy-start.6 = (f32[20,640]{1,0:T(8,128)S(1)}, f32[20,640]{1,0:T(8,128)}, u32[]{:S(2)}) copy-start(f32[20,640]{1,0:T(8,128)} %param.13) | copy-start | bytes 153604
  78.5 1.3 copy-start.1
  80.0 48.5 %collective-permute-start.6 = (f32[33,1,640]{2,1,0:T(1,128)S(1)}, f32[33,1,640]{2,1,0:T(1,128)S(1)}, u32[]{:S(2)}, u32[]{:S(2)}) collective-permute-start(f32[33,1,640]{2,1,0:T(1,128)S(1)} %get-tuple-element.38), channel_id=1, source_target_pairs={{0,8},{8,16},{16,24},{24,32},{32,40},{40,48},{48,56},{56,64},{64,7... | collective-permute-start | bytes 253448 | tf_op jit(solution)/shard_map/ppermute | solution.py:16
  81.9 46.6 %collective-permute-start.7 = (f32[33,1,640]{2,1,0:T(1,128)S(1)}, f32[33,1,640]{2,1,0:T(1,128)S(1)}, u32[]{:S(2)}, u32[]{:S(2)}) collective-permute-start(f32[33,1,640]{2,1,0:T(1,128)S(1)} %get-tuple-element.37), channel_id=1, source_target_pairs={{8,0},{16,8},{24,16},{32,24},{40,32},{48,40},{56,48},{64,56},{72,6... | collective-permute-start | bytes 253448 | tf_op jit(solution)/shard_map/ppermute | solution.py:18
  130.4 36.6 %copy-start.2 = (f32[32,20,640]{2,1,0:T(8,128)S(1)}, f32[32,20,640]{2,1,0:T(8,128)}, u32[]{:S(2)}) copy-start(f32[32,20,640]{2,1,0:T(8,128)} %copy-done.1) | copy-start | bytes 4915204
  131.4 35.6 %collective-permute-start.8 = (f32[33,22,1]{2,1,0:T(8,128)}, f32[33,22,1]{2,1,0:T(8,128)S(1)}, u32[]{:S(2)}, u32[]{:S(2)}) collective-permute-start(f32[33,22,1]{2,1,0:T(8,128)} %get-tuple-element.36), channel_id=1, source_target_pairs={{0,1},{1,2},{2,3},{3,4},{4,5},{5,6},{6,7},{7,0},{8,9},{9,10},{10,1... | collective-permute-start | bytes 8720 | tf_op jit(solution)/shard_map/ppermute | solution.py:16
  134.7 32.3 %collective-permute-start.9 = (f32[33,22,1]{2,1,0:T(8,128)}, f32[33,22,1]{2,1,0:T(8,128)S(1)}, u32[]{:S(2)}, u32[]{:S(2)}) collective-permute-start(f32[33,22,1]{2,1,0:T(8,128)} %get-tuple-element.35), channel_id=1, source_target_pairs={{1,0},{2,1},{3,2},{4,3},{5,4},{6,5},{7,6},{0,7},{9,8},{10,9},{11,1... | collective-permute-start | bytes 8720 | tf_op jit(solution)/shard_map/ppermute | solution.py:18
  142.1 68.2 %all-to-all-start = ((bf16[4,256,20]{2,0,1:T(4,128)(2,1)}), bf16[4,256,20]{2,0,1:T(4,128)(2,1)S(1)}, u32[]{:S(2)}, u32[]{:S(2)}) async-start(bf16[4,256,20]{2,0,1:T(4,128)(2,1)} %copy.44), calls=%async_computation | async-start | bytes 524288 | tf_op jit(solution)/shard_map/all_to_all | solution.py:67
  167.0 0.8 copy-start.7
where the time goes:
time: 215 us
  starting transfers between devices  68.7 us (32%)
  blocking collectives  57.8 us (27%)
  waiting for transfers between devices  51.7 us (24%)
  other arithmetic  20 us (9%)
  local copies, waits for them, and re-layouts  10.7 us (5%)
  matrix products  4.06 us (2%)
    unnamed x1, blocking collectives  38.2 us
    all_to_all x1, waiting for transfers between devices, shards(): lax.all_to_all(fourier, ('grp', 'lat'), split_axis=1, concat_axis=2, tile...  34.6 us
    ppermute x5, starting transfers between devices, with_halo(): lax.ppermute(head, axis, [((i + 1) % count, i) for i in range(count)])  27.4 us
    all_to_all x1, starting transfers between devices, shards(): lax.all_to_all(fourier, ('grp', 'lat'), split_axis=1, concat_axis=2, tile...  24.9 us
    all_gather x1, blocking collectives, shards(): near_tiles = lax.all_gather(lon_near, 'grp', axis=0, tiled=True)  19.6 us
    ppermute x5, starting transfers between devices, with_halo(): lax.ppermute(tail, axis, [(i, (i + 1) % count) for i in range(count)])  16.4 us
    add x2, other arithmetic, relax(): return centre + diffusion * centre_wet * laplace_sum  12.6 us
    ppermute x5, waiting for transfers between devices, with_halo(): lax.ppermute(tail, axis, [(i, (i + 1) % count) for i in range(count)])  10.7 us
  transfers between devices with their start and end apart: 11, of which 5 were waited for; matrix products, arithmetic and copies ran while one was open for 7% of the time, Pallas kernels for 0%

commit v1 on v0

v1 whole, which is shorter than its diff:
```python
import functools
import math

import jax
import jax.numpy as jnp
import numpy as np
from jax import lax
from jax.experimental import pallas as pl
from jax.experimental.pallas import tpu as pltpu
from jax.sharding import PartitionSpec as P

F32 = jnp.float32
BF16 = jnp.bfloat16
I32 = jnp.int32
NT = (((1,), (1,)), ((), ()))
TN = (((0,), (0,)), ((), ()))

ROW_LIST = 40
ROW_EDGE = 48
ROW_WGT = 64
ROW_SENT = 80
SLOT_ROWS = 184
WIDE = 768
EXTRA = 8


def iota(shape, dim):
    return lax.broadcasted_iota(I32, shape, dim)


def onehot(cond):
    return jnp.where(cond, 1.0, 0.0).astype(BF16)


def mm(a, b, dims=(((1,), (0,)), ((), ())), precision=None):
    return lax.dot_general(a, b, dims, preferred_element_type=F32, precision=precision)


def split_hi_lo(x):
    hi = x.astype(BF16).astype(F32)
    return hi, x - hi


def pack_kernel(pos_ref, list_ref, cos_ref, sin_ref, grid_ref, sent_ref, wet_ref, diff_ref, wgt_ref, out_ref):
    me_lon = pos_ref[1]
    turn = (iota((128, 1), 0) * me_lon) & 7
    half = math.sqrt(0.5)

    def eighth(k):
        values = (1.0, half, 0.0, -half, -1.0, -half, 0.0, half)
        out = jnp.zeros((128, 1), F32)
        for i, v in enumerate(values):
            out = jnp.where(((turn + k) & 7) == i, v, out)
        return out

    cos_t, sin_t = eighth(0), eighth(6)
    cos0, sin0 = cos_ref[...], sin_ref[...]
    cos_m = cos_t * cos0 - sin_t * sin0
    sin_m = -(sin_t * cos0 + cos_t * sin0)
    parts = []
    for g in range(4):
        parts += [cos_m[32 * g : 32 * g + 32], sin_m[32 * g : 32 * g + 32]]
    basis = jnp.concatenate(parts, axis=0).astype(BF16)
    state = grid_ref[...].reshape(640, 640)
    sums = mm(state, basis, NT).astype(BF16)
    rho = iota((640, 1), 0)
    jh = (rho >= 320).astype(I32)
    rem = rho - 320 * jh
    tt = (rem * 205) >> 13
    rem = rem - 40 * tt
    j2 = (rem >= 20).astype(I32)
    source = (rem - 20 * j2) * 32 + 4 * tt + 2 * jh + j2
    order = onehot(iota((640, 640), 1) == source)
    moved = mm(order, sums)
    low, high = moved[:320], moved[320:]
    row8, lane8 = iota((8, 128), 0), iota((8, 128), 1)
    listing = jnp.zeros((8, 128), F32)
    for e in range(8):
        for c in range(3):
            listing = jnp.where((row8 == e) & (lane8 == c), list_ref[3 * e + c].astype(F32), listing)
    for g in range(4):
        tile = jnp.concatenate([low[:, 64 * g : 64 * g + 64], high[:, 64 * g : 64 * g + 64]], axis=1)
        for t in range(8):
            block = jnp.concatenate([tile[40 * t : 40 * t + 40], listing], axis=0)
            out_ref[g * 8 + t, 0:48, :] = block.astype(BF16)
    sent = sent_ref[...].astype(BF16)
    pad = jnp.zeros((12, 128), BF16)
    spread = jnp.zeros((104, 128), F32)
    for c in range(5):
        pick = onehot(iota((104, 32), 0) == iota((104, 32), 1) + 20 * c) * onehot(iota((104, 32), 1) < 20)
        spread += mm(pick, jnp.concatenate([sent[:, 128 * c : 128 * c + 128].astype(F32), pad.astype(F32)], axis=0).astype(BF16))
    spread = spread.astype(BF16)
    wet = wet_ref[...].astype(F32)
    dif = diff_ref[...] * wet
    pad12 = jnp.zeros((12, 128), F32)
    edges = []
    for side in range(2):
        base = 0 if side == 0 else 512
        lane0 = 0 if side == 0 else 126
        acc = jnp.zeros((16, 128), F32)
        for k in range(6):
            if k < 5:
                src = grid_ref[4 * k : 4 * k + 4, :, base : base + 128].reshape(128, 128)
            else:
                hi, lo = split_hi_lo(dif[:, base : base + 128])
                src = jnp.concatenate(
                    [wet[:, base : base + 128], pad12, hi, pad12, lo, pad12, jnp.zeros((32, 128), F32)], axis=0
                ).astype(BF16)
            r16, l16 = iota((16, 128), 0), iota((16, 128), 1)
            pick = onehot(((r16 == k) & (l16 == lane0)) | ((r16 == 8 + k) & (l16 == lane0 + 1)))
            acc += mm(pick, src, NT)
        edges.append(acc)
    wgt = []
    for side in range(2):
        pieces = []
        for i in range(2):
            r = i if side == 0 else 126 + i
            rows = jnp.zeros((8, 128), F32)
            for e in range(8):
                rows = jnp.where(row8 == e, wgt_ref[e, (r // 16) * 16 : (r // 16) * 16 + 16, :].astype(F32)[r % 16 : r % 16 + 1], rows)
            pieces.append(rows)
        wgt.append(jnp.concatenate(pieces, axis=0))
    left = jnp.concatenate([edges[0], wgt[0]], axis=0)
    right = jnp.concatenate([edges[1], wgt[1]], axis=0)
    for t in range(8):
        to_left = ((me_lon + 7) & 7) == t
        block = jnp.where(to_left, left, right).astype(BF16)
        for g in range(4):
            out_ref[g * 8 + t, ROW_EDGE:ROW_SENT, :] = block
            out_ref[g * 8 + t, ROW_SENT:SLOT_ROWS, :] = spread


def turn_kernel(recv_ref, out_ref):
    norm = np.float32(1.0 / math.sqrt(5120.0))
    sums = []
    for g in range(3):
        acc = recv_ref[g * 8, 0:48, :].astype(F32)
        for t in range(1, 8):
            acc += recv_ref[g * 8 + t, 0:48, :].astype(F32)
        sums.append(acc[0:40])
    stack = (jnp.concatenate(sums + [jnp.zeros((8, 128), F32)], axis=0) * norm).astype(BF16)
    out = jnp.zeros((256, 128), F32)
    for j2 in range(2):
        lane = iota((128, 128), 0)
        g = (lane >= 20).astype(I32) + (lane >= 40).astype(I32)
        pick = onehot((iota((128, 128), 1) == lane + 20 * g + 20 * j2) & (lane < 60))
        lined = mm(pick, stack).astype(BF16)
        rho, lam = iota((256, 128), 0), iota((256, 128), 1)
        want = ((rho >> 2) & 1) * 64 + (rho & 1) * 32 + (rho >> 3)
        place = onehot((((rho >> 1) & 1) == j2) & (lam == want))
        out += mm(place, lined, NT)
    out_ref[...] = out.astype(BF16)


def remap_kernel(pos_ref, list_ref, recv_ref, wgt_ref, wet_ref, diff_ref, grid_ref,
                 rec_ref, tail_ref, planes_ref, up_ref, down_ref):
    me_grp, me_lon = pos_ref[0], pos_ref[1]
    slot_l = me_grp * 8 + ((me_lon + 7) & 7)
    slot_r = me_grp * 8 + ((me_lon + 1) & 7)
    row8 = iota((8, 1), 0)

    def field(c):
        out = jnp.zeros((8, 1), I32)
        for e in range(8):
            out = jnp.where(row8 == e, list_ref[3 * e + c], out)
        return out

    def ids(k, s, centre):
        h = (k >= 3).astype(I32) + (k >= 6).astype(I32) + (k >= 9).astype(I32)
        lon = (centre + k - 3 * h + 7) & 7
        row = (s * 205) >> 10
        return h * 8 + lon, (s - 5 * row) * 20 + row

    lists = [(field(0), field(1), field(2))]
    for slot in (slot_l, slot_r):
        rows = recv_ref[slot, 32:48, :].astype(F32)[8:16].astype(I32)
        lists.append((rows[:, 0:1], rows[:, 1:2], rows[:, 2:3]))
    pairs = [ids(k, s, me_lon + shift) for (k, s, _), shift in zip(lists, (0, 7, 1))]
    slot_id = jnp.concatenate([p[0] for p in pairs], axis=0)
    block_id = jnp.concatenate([p[1] for p in pairs], axis=0)
    in_block = jnp.where(iota((24, 104), 1) == block_id, 1.0, 0.0)
    source = jnp.zeros((24, 128), F32)
    for slot in range(32):
        pick = jnp.where(slot_id == slot, in_block, 0.0).astype(BF16)
        source += mm(pick, recv_ref[slot, ROW_SENT:SLOT_ROWS, :])
    own = source[0:8].astype(BF16)
    prod = jnp.zeros((8, 128), F32)
    for e in range(8):
        prod = jnp.where(row8 == e, mm(own, wgt_ref[e], NT), prod)
    target = lists[0][2]
    trow = (target * 205) >> 10
    place = jnp.where(iota((8, 256), 1) == (target - 5 * trow) * 32 + trow, 1.0, 0.0)
    placed = mm(place, prod, TN, lax.Precision.HIGHEST)
    tiles = [placed[32 * c : 32 * c + 20] for c in range(5)]
    received = jnp.concatenate(tiles, axis=1)
    rec_ref[...] = received
    lane = iota((8, 128), 1)
    values, spots = [], []
    for n, (slot, lane0, col) in enumerate(((slot_l, 126, 4), (slot_r, 0, 0))):
        rows = recv_ref[slot, ROW_WGT:ROW_SENT, :].astype(F32)
        src = source[8 + 8 * n : 16 + 8 * n]
        v0 = jnp.sum(rows[0:8] * src, axis=1, keepdims=True)
        v1 = jnp.sum(rows[8:16] * src, axis=1, keepdims=True)
        values.append(jnp.where(lane == lane0, v0, 0.0) + jnp.where(lane == lane0 + 1, v1, 0.0))
        goal = lists[1 + n][2]
        grow = (goal * 205) >> 10
        spots.append(jnp.where((iota((8, 128), 1) == grow) & (goal - 5 * grow == col), 1.0, 0.0))
    rec_tail = mm(jnp.concatenate(spots, axis=0), jnp.concatenate(values, axis=0), TN, lax.Precision.HIGHEST)[0:20]
    edge = jnp.concatenate(
        [recv_ref[slot_l, ROW_EDGE:ROW_WGT, :].astype(F32), recv_ref[slot_r, ROW_EDGE:ROW_WGT, :].astype(F32)], axis=0
    ).astype(BF16)
    r32, l32 = iota((32, 128), 0), iota((32, 128), 1)

    def tail_of(k):
        pick = onehot(
            ((r32 == k) & (l32 == 126)) | ((r32 == 8 + k) & (l32 == 127))
            | ((r32 == 16 + k) & (l32 == 0)) | ((r32 == 24 + k) & (l32 == 1))
        )
        return mm(edge, pick, TN)

    for k in range(5):
        tail_ref[4 * k : 4 * k + 4] = tail_of(k).reshape(4, 32, 128).astype(BF16)
    last = tail_of(5)
    wet = jnp.concatenate([wet_ref[...].astype(F32), last[0:20]], axis=1)
    dif = jnp.concatenate([diff_ref[...] * wet_ref[...].astype(F32), last[32:52] + last[64:84]], axis=1)
    force = wet * jnp.concatenate([received, rec_tail], axis=1)
    planes_ref[0] = wet
    planes_ref[1] = dif
    planes_ref[2] = force
    dhi, dlo = split_hi_lo(dif)
    fhi, flo = split_hi_lo(force)
    rowx = iota((EXTRA, WIDE), 0)
    for ref, first in ((up_ref, 0), (down_ref, 18)):
        for i in range(2):
            r = first + i
            ref[i, 0:32, 0:640] = grid_ref[r]
            ref[i, 0:32, 640:WIDE] = tail_ref[r]
            extra = jnp.zeros((EXTRA, WIDE), F32)
            for n, x in enumerate((wet, dhi, dlo, fhi, flo)):
                extra = jnp.where(rowx == n, x[r : r + 1], extra)
            ref[i, 32 : 32 + EXTRA, :] = extra.astype(BF16)


def step_kernel(grid_ref, tail_ref, planes_ref, above_ref, below_ref, out_ref, q_ref, u_ref, wet_ref, dif_ref, c_ref):
    level0 = iota((32, WIDE), 0) == 0

    def load(r, cells, wet, dif, force):
        cells = jnp.where(level0, cells + force, cells)
        wet_ref[r] = jnp.broadcast_to(wet, (8, WIDE))
        dif_ref[r] = jnp.broadcast_to(dif, (8, WIDE))
        q_ref[r] = cells
        u_ref[r] = cells * wet

    for i in range(2):
        for ref, r in ((above_ref, i), (below_ref, 22 + i)):
            extra = ref[i, 32 : 32 + EXTRA, :].astype(F32) if EXTRA == 16 else ref[i, 32:40, :].astype(F32)
            load(r, ref[i, 0:32, :].astype(F32), extra[0:1], extra[1:2] + extra[2:3], extra[3:4] + extra[4:5])
    for r in range(20):
        cells = jnp.concatenate([grid_ref[r].astype(F32), tail_ref[r].astype(F32)], axis=1)
        load(r + 2, cells, planes_ref[0, r : r + 1, :], planes_ref[1, r : r + 1, :], planes_ref[2, r : r + 1, :])

    def sides(x):
        return pltpu.roll(x, 1, axis=1) + pltpu.roll(x, WIDE - 1, axis=1)

    def coef(r, carry):
        near = wet_ref[r - 1] + wet_ref[r + 1] + sides(wet_ref[r])
        c_ref[r] = 1.0 - dif_ref[r] * near
        return carry

    lax.fori_loop(1, 23, coef, 0)

    def four(x):
        return jnp.concatenate([x] * 4, axis=0)

    def first(r, prev):
        here = u_ref[r]
        total = sides(here) + prev + u_ref[r + 1]
        q = q_ref[r] * four(c_ref[r]) + four(dif_ref[r]) * total
        q_ref[r] = q
        u_ref[r] = q * four(wet_ref[r])
        return here

    lax.fori_loop(1, 23, first, u_ref[0])

    def second(r, carry):
        total = sides(u_ref[r]) + u_ref[r - 1] + u_ref[r + 1]
        q = q_ref[r] * four(c_ref[r]) + four(dif_ref[r]) * total
        out_ref[r - 2] = q[:, 0:640]
        return carry

    lax.fori_loop(2, 22, second, 0)


VMEM = pl.BlockSpec(memory_space=pltpu.VMEM)
SMEM = pl.BlockSpec(memory_space=pltpu.SMEM)
PARAMS = pltpu.CompilerParams(vmem_limit_bytes=40 * 1024 * 1024)


def call(kernel, name, smem, vmem, outs, scratch=()):
    flat = [jax.ShapeDtypeStruct(s, d) for s, d in outs]
    return pl.pallas_call(
        kernel,
        name=name,
        out_shape=flat if len(flat) > 1 else flat[0],
        in_specs=[SMEM] * len(smem) + [VMEM] * len(vmem),
        out_specs=[VMEM] * len(flat) if len(flat) > 1 else VMEM,
        scratch_shapes=list(scratch),
        compiler_params=PARAMS,
    )(*smem, *vmem)


def trig_tables():
    phase = np.arange(128)[:, None] * np.arange(640)[None, :] % 5120
    angle = 2.0 * np.pi / 5120.0 * phase
    return np.cos(angle).astype(np.float32), np.sin(angle).astype(np.float32)


def shards(grid_state, legendre, sent_field, wet_mask, diffusivity, remap_blocks, remap_weights):
    rows = grid_state.transpose(1, 0, 2)
    pos = jnp.stack([lax.axis_index("grp"), lax.axis_index("lon")]).astype(I32)
    listing = remap_blocks.reshape(24)
    weights = remap_weights[0, 0]
    cos0, sin0 = trig_tables()
    packed = call(
        pack_kernel, "pack", (pos, listing),
        (jnp.asarray(cos0), jnp.asarray(sin0), rows, sent_field, wet_mask, diffusivity, weights),
        [((32, SLOT_ROWS, 128), BF16)],
    )
    plane = lax.all_to_all(packed, ("grp", "lon"), 0, 0, tiled=True)
    turned = call(turn_kernel, "turn", (), (plane,), [((256, 128), BF16)])
    waves = lax.all_to_all(turned.reshape(32, 8, 128), "lat", 0, 0, tiled=True)
    received, tail, planes, up, down = call(
        remap_kernel, "remap", (pos, listing), (plane, weights, wet_mask, diffusivity, rows),
        [((20, 640), F32), ((20, 32, 128), BF16), ((3, 20, WIDE), F32),
         ((2, 32 + EXTRA, WIDE), BF16), ((2, 32 + EXTRA, WIDE), BF16)],
    )
    bands = lax.axis_size(("grp", "lat"))
    below = lax.ppermute(up, ("grp", "lat"), [((i + 1) % bands, i) for i in range(bands)])
    above = lax.ppermute(down, ("grp", "lat"), [(i, (i + 1) % bands) for i in range(bands)])
    stepped = call(
        step_kernel, "step", (), (rows, tail, planes, above, below),
        [((20, 32, 640), F32)],
        scratch=[pltpu.VMEM((24, 32, WIDE), F32), pltpu.VMEM((24, 32, WIDE), F32),
                 pltpu.VMEM((24, 8, WIDE), F32), pltpu.VMEM((24, 8, WIDE), F32), pltpu.VMEM((24, 8, WIDE), F32)],
    )
    grid_next = stepped.transpose(1, 0, 2)
    left = waves[:, :, :60].reshape(32, 8, 3, 20).transpose(1, 2, 0, 3).reshape(8, 1920)
    spectral = mm(left, legendre[0]).reshape(1, 4, 2, 1280)
    return spectral, received, grid_next


def solution(mesh):
    in_specs = (
        P(None, ("grp", "lat"), "lon"),
        P(("grp", "lat"), None, None),
        P(("grp", "lat"), "lon"),
        P(("grp", "lat"), "lon"),
        P(("grp", "lat"), "lon"),
        P(("grp", "lat"), "lon", None, None),
        P(("grp", "lat"), "lon", None, None, None),
    )
    out_specs = (
        P(("grp", "lat"), "lon", None, None),
        P(("grp", "lat"), "lon"),
        P(None, ("grp", "lat"), "lon"),
    )
    return jax.shard_map(shards, mesh=mesh, in_specs=in_specs, out_specs=out_specs, check_vma=False)
```

time: 215 us -> 100 us (0.47)
  waiting for transfers between devices: 51.7 us -> 6.51 us
  starting transfers between devices: 68.7 us -> 26.8 us
  other arithmetic: 20 us -> 0.07 us
  blocking collectives: 57.8 us -> 39.3 us
  Pallas kernels: 0 us -> 14.5 us
    all_to_all x0 -> x1, blocking collectives: none -> 39.3 us  [shards(): plane = lax.all_to_all(packed, ('grp', 'lon'), 0, 0, tiled=True)]
    unnamed x1 -> x0, blocking collectives: 38.2 us -> none
    ppermute x10 -> x2, starting transfers between devices: 43.8 us -> 6.76 us  [the longest x1 3.64 us: shards(): lax.ppermute(up, ('grp', 'lat'), [((i + 1) % bands, i) for i in range(ban...]
    all_to_all x1, waiting for transfers between devices: 34.6 us -> 3.23 us  [shards(): waves = lax.all_to_all(turned.reshape(32, 8, 128), 'lat', 0, 0, tiled=True)]
    all_gather x1 -> x0, blocking collectives: 19.6 us -> none  [shards(): near_tiles = lax.all_gather(lon_near, 'grp', axis=0, tiled=True)]
    pallas_call x0 -> x4, Pallas kernels: none -> 14.5 us  [call(): pl.pallas_call(kernel, name=name, out_shape=flat if len(flat) > 1 else fl...]
    ppermute x10 -> x2, waiting for transfers between devices: 17.1 us -> 3.28 us  [the longest x1 3.28 us: shards(): lax.ppermute(down, ('grp', 'lat'), [(i, (i + 1) % bands) for i in range(b...]
    add x3 -> x0, other arithmetic: 12.6 us -> none  [the longest x2 12.6 us: relax(): return centre + diffusion * centre_wet * laplace_sum]
  transfers between devices with their start and end apart: 11 -> 3, of which waited for: 5 -> 2; matrix products, arithmetic and copies ran while one was open for 7% -> 0% of each run, Pallas kernels for 0% -> 11%
where the time goes in v1:
time: 100 us; the launch traced here: 99.9 us
  blocking collectives  39.3 us (39%)
  starting transfers between devices  26.8 us (27%)
  Pallas kernels  14.5 us (14%)
  local copies, waits for them, and re-layouts  8.79 us (9%)
  waiting for transfers between devices  6.51 us (7%)
  matrix products  3.18 us (3%)
    all_to_all x1, blocking collectives, shards(): plane = lax.all_to_all(packed, ('grp', 'lon'), 0, 0, tiled=True)  39.3 us
    all_to_all x1, starting transfers between devices, shards(): waves = lax.all_to_all(turned.reshape(32, 8, 128), 'lat', 0, 0, tiled=True)  20 us
    pallas_call x4, Pallas kernels, call(): pl.pallas_call(kernel, name=name, out_shape=flat if len(flat) > 1 else fl...  14.5 us
    unnamed x25, local copies, waits for them, and re-layouts  8.12 us
    ppermute x1, starting transfers between devices, shards(): lax.ppermute(up, ('grp', 'lat'), [((i + 1) % bands, i) for i in range(ban...  3.64 us
    ppermute x1, waiting for transfers between devices, shards(): lax.ppermute(down, ('grp', 'lat'), [(i, (i + 1) % bands) for i in range(b...  3.28 us
    all_to_all x1, waiting for transfers between devices, shards(): waves = lax.all_to_all(turned.reshape(32, 8, 128), 'lat', 0, 0, tiled=True)  3.23 us
    dot_general x1, matrix products, mm(): lax.dot_general(a, b, dims, preferred_element_type=F32, precision=precision)  3.18 us
  transfers between devices with their start and end apart: 3, of which 2 were waited for; matrix products, arithmetic and copies ran while one was open for 0% of the time, Pallas kernels for 11%

profile of v1, /device:TPU:1, one launch (start us, length us, event | category | flops | bytes accessed | tf_op | source)
XLA Modules:
  0.0 99.9 jit_solution(11548177604286247735)
XLA Ops:
  0.6 0.8 copy.19
  1.4 0.1 reshape.24.list_ref
  1.5 0.1 pad_add_fusion.pos_ref
  1.5 0.0 copy-start
  1.6 1.1 %copy-done = bf16[32,20,640]{2,0,1:T(8,128)(2,1)S(1)} copy-done((bf16[32,20,640]{2,0,1:T(8,128)(2,1)S(1)}, bf16[32,20,640]{2,0,1:T(8,128)(2,1)}, u32[]{:S(2)}) %copy-start) | copy-done | bytes 819224
  2.7 0.0 copy-start.2
  2.7 0.9 copy-done.2
  3.6 1.0 copy-done.4
  4.6 1.0 copy-done.5
  5.6 0.8 copy-done.6
  6.4 0.8 copy-done.8
  7.3 0.8 copy-done.10
  8.1 2.1 %pack.1 = bf16[32,184,128]{2,1,0:T(8,128)(2,1)S(1)} custom-call(s32[2]{0:T(128)S(1)} %pad_add_fusion.pos_ref, s32[24]{0:T(128)S(1)} %reshape.24.list_ref, f32[128,640]{1,0:T(8,128)S(1)} %copy-done.5, f32[128,640]{1,0:T(8,128)S(1)} %copy-done.4, bf16[20,32,640]{2,1,0:T(8,128)(2,1)S(1)} %bitcast.22, f32[20,640]{1,0:T(8,128)S(1)} %copy-done.10, ...), custom_call_target="tpu_custom_call" | custom-call | tf_op jit(solution)/shard_map/pack/pallas_call | solution.py:301
  10.2 39.3 %all_to_all.10.recv_ref = bf16[32,184,128]{2,1,0:T(8,128)(2,1)S(1)} all-to-all(bf16[32,184,128]{2,1,0:T(8,128)(2,1)S(1)} %pack.1), channel_id=1, replica_groups=mesh['grp'=4,'lat'=32,'lon'=8] {'grp','lon'}, dimensions={0} | all-to-all | bytes 3014656 | tf_op jit(solution)/shard_map/all_to_all | solution.py:329
  49.5 1.0 turn.1
  50.5 20.0 %all-to-all-start.1 = ((bf16[32,8,128]{2,1,0:T(8,128)(2,1)}), bf16[32,8,128]{2,1,0:T(8,128)(2,1)S(1)}, u32[]{:S(2)}, u32[]{:S(2)}) async-start(bf16[32,8,128]{2,1,0:T(8,128)(2,1)} %bitcast.4), calls=%async_computation.1 | async-start | bytes 131072 | tf_op jit(solution)/shard_map/all_to_all | solution.py:331
  70.5 0.0 copy-done.1
  70.5 0.0 copy-done.3
  70.5 0.0 copy-done.7
  70.5 0.0 copy-done.9
  70.5 2.6 %remap.1 = (f32[20,640]{1,0:T(8,128)}, bf16[20,32,128]{2,1,0:T(8,128)(2,1)S(1)}, f32[3,20,768]{2,1,0:T(8,128)S(1)}, bf16[2,40,768]{2,1,0:T(8,128)(2,1)S(1)}, bf16[2,40,768]{2,1,0:T(8,128)(2,1)S(1)}) custom-call(s32[2]{0:T(128)S(1)} %pad_add_fusion.pos_ref, s32[24]{0:T(128)S(1)} %reshape.24.list_ref, bf16[32,184,128]{2,1,0:T(8,128)(2,1)S(1)} %all_to_all.10.recv_ref, ...), custom_call_target="tpu_custom_call" | custom-call | tf_op jit(solution)/shard_map/remap/pallas_call | solution.py:301
  73.1 3.1 %collective-permute-start = (bf16[2,40,768]{2,1,0:T(8,128)(2,1)S(1)}, bf16[2,40,768]{2,1,0:T(8,128)(2,1)S(1)}, u32[]{:S(2)}, u32[]{:S(2)}) collective-permute-start(bf16[2,40,768]{2,1,0:T(8,128)(2,1)S(1)} %get-tuple-element.11), channel_id=1, source_target_pairs={{0,8},{8,16},{16,24},{24,32},{32,40},{40,48},{48,56},{56,64},{64,7... | collective-permute-start | bytes 368648 | tf_op jit(solution)/shard_map/ppermute | solution.py:339
  76.2 3.6 %collective-permute-start.1 = (bf16[2,40,768]{2,1,0:T(8,128)(2,1)S(1)}, bf16[2,40,768]{2,1,0:T(8,128)(2,1)S(1)}, u32[]{:S(2)}, u32[]{:S(2)}) collective-permute-start(bf16[2,40,768]{2,1,0:T(8,128)(2,1)S(1)} %get-tuple-element.12), channel_id=1, source_target_pairs={{8,0},{16,8},{24,16},{32,24},{40,32},{48,40},{56,48},{64,56},{72,6... | collective-permute-start | bytes 368648 | tf_op jit(solution)/shard_map/ppermute | solution.py:338
  79.9 3.3 %collective-permute-done.above_ref = bf16[2,40,768]{2,1,0:T(8,128)(2,1)S(1)} collective-permute-done((bf16[2,40,768]{2,1,0:T(8,128)(2,1)S(1)}, bf16[2,40,768]{2,1,0:T(8,128)(2,1)S(1)}, u32[]{:S(2)}, u32[]{:S(2)}) %collective-permute-start) | collective-permute-done | bytes 122912 | tf_op jit(solution)/shard_map/ppermute | solution.py:339
  83.2 0.0 collective-permute-done.1.below_ref
  83.2 8.9 %step.1 = f32[20,32,640]{2,1,0:T(8,128)} custom-call(bf16[20,32,640]{2,1,0:T(8,128)(2,1)S(1)} %bitcast.24, bf16[20,32,128]{2,1,0:T(8,128)(2,1)S(1)} %get-tuple-element.9.tail_ref, f32[3,20,768]{2,1,0:T(8,128)S(1)} %get-tuple-element.10.planes_ref, bf16[2,40,768]{2,1,0:T(8,128)(2,1)S(1)} %collective-permute-done.above_ref, ...), custom_call_target="tpu_custom_call" | custom-call | tf_op jit(solution)/shard_map/step/pallas_call | solution.py:301
  92.0 3.2 %all-to-all-done.1 = bf16[32,8,128]{2,1,0:T(8,128)(2,1)S(1)} async-done(((bf16[32,8,128]{2,1,0:T(8,128)(2,1)}), bf16[32,8,128]{2,1,0:T(8,128)(2,1)S(1)}, u32[]{:S(2)}, u32[]{:S(2)}) %all-to-all-start.1) | async-done | bytes 65568 | tf_op jit(solution)/shard_map/all_to_all | solution.py:331
  95.3 0.2 copy.24
  95.4 0.3 copy.21
  95.7 0.3 reshape.27
  96.0 3.2 %fusion.2 = f32[1,4,2,1280]{3,1,2,0:T(4,128)S(1)} fusion(bf16[1,1920,1280]{2,1,0:T(8,128)(2,1)} %param.10, bf16[4,2,1920]{2,1,0:T(2,128)(2,1)S(1)} %reshape.27), kind=kOutput, calls=%fused_computation.2 | convolution fusion | flops 39321600 | bytes 4986880 | tf_op jit(solution)/shard_map/dot_general | solution.py:36
  99.2 0.7 copy.23
  (9 shorter events, 0.0 us)
Async XLA Ops:
  1.5 1.1 %copy-start = (bf16[32,20,640]{2,0,1:T(8,128)(2,1)S(1)}, bf16[32,20,640]{2,0,1:T(8,128)(2,1)}, u32[]{:S(2)}) copy-start(bf16[32,20,640]{2,0,1:T(8,128)(2,1)} %param.9) | copy-start | bytes 2457604
  2.7 0.9 copy-start.2
  3.6 1.0 copy-start.4
  4.6 1.0 copy-start.5
  5.6 0.8 copy-start.6
  6.4 0.8 copy-start.8
  7.3 0.8 copy-start.10
  8.1 62.4 %copy-start.1 = (bf16[32,20,640]{2,0,1:T(8,128)(2,1)S(1)}, bf16[32,20,640]{2,0,1:T(8,128)(2,1)}, u32[]{:S(2)}) copy-start(bf16[32,20,640]{2,0,1:T(8,128)(2,1)} %param.9) | copy-start | bytes 2457604
  8.1 62.4 %copy-start.3 = (bf16[1,1,8,128,128]{4,3,2,1,0:T(8,128)(2,1)S(1)}, bf16[1,1,8,128,128]{4,3,2,1,0:T(8,128)(2,1)}, u32[]{:S(2)}) copy-start(bf16[1,1,8,128,128]{4,3,2,1,0:T(8,128)(2,1)} %param.15) | copy-start | bytes 786436
  8.1 62.4 %copy-start.7 = (s32[20,640]{1,0:T(8,128)S(1)}, s32[20,640]{1,0:T(8,128)}, u32[]{:S(2)}) copy-start(s32[20,640]{1,0:T(8,128)} %wet_ref.3) | copy-start | bytes 153604
  8.1 62.4 %copy-start.9 = (f32[20,640]{1,0:T(8,128)S(1)}, f32[20,640]{1,0:T(8,128)}, u32[]{:S(2)}) copy-start(f32[20,640]{1,0:T(8,128)} %diff_ref.3) | copy-start | bytes 153604
  50.5 44.8 %all-to-all-start.1 = ((bf16[32,8,128]{2,1,0:T(8,128)(2,1)}), bf16[32,8,128]{2,1,0:T(8,128)(2,1)S(1)}, u32[]{:S(2)}, u32[]{:S(2)}) async-start(bf16[32,8,128]{2,1,0:T(8,128)(2,1)} %bitcast.4), calls=%async_computation.1 | async-start | bytes 131072 | tf_op jit(solution)/shard_map/all_to_all | solution.py:331
  73.1 10.1 %collective-permute-start = (bf16[2,40,768]{2,1,0:T(8,128)(2,1)S(1)}, bf16[2,40,768]{2,1,0:T(8,128)(2,1)S(1)}, u32[]{:S(2)}, u32[]{:S(2)}) collective-permute-start(bf16[2,40,768]{2,1,0:T(8,128)(2,1)S(1)} %get-tuple-element.11), channel_id=1, source_target_pairs={{0,8},{8,16},{16,24},{24,32},{32,40},{40,48},{48,56},{56,64},{64,7... | collective-permute-start | bytes 368648 | tf_op jit(solution)/shard_map/ppermute | solution.py:339
  76.2 6.9 %collective-permute-start.1 = (bf16[2,40,768]{2,1,0:T(8,128)(2,1)S(1)}, bf16[2,40,768]{2,1,0:T(8,128)(2,1)S(1)}, u32[]{:S(2)}, u32[]{:S(2)}) collective-permute-start(bf16[2,40,768]{2,1,0:T(8,128)(2,1)S(1)} %get-tuple-element.12), channel_id=1, source_target_pairs={{8,0},{16,8},{24,16},{32,24},{40,32},{48,40},{56,48},{64,56},{72,6... | collective-permute-start | bytes 368648 | tf_op jit(solution)/shard_map/ppermute | solution.py:338

commit v2 on v1

v2 whole, which is shorter than its diff:
```python
import functools
import math

import jax
import jax.numpy as jnp
import numpy as np
from jax import lax
from jax.experimental import pallas as pl
from jax.experimental.pallas import tpu as pltpu
from jax.sharding import PartitionSpec as P

F32 = jnp.float32
BF16 = jnp.bfloat16
I32 = jnp.int32
NT = (((1,), (1,)), ((), ()))
TN = (((0,), (0,)), ((), ()))

WIDE = 768
ROW_EDGE = 48
ROW_WGT = 64
ROW_SENT = 80
SLOT_ROWS = 184


def iota(shape, dim):
    return lax.broadcasted_iota(I32, shape, dim)


def onehot(cond):
    return jnp.where(cond, 1.0, 0.0).astype(BF16)


def mm(a, b, dims=(((1,), (0,)), ((), ())), precision=None):
    return lax.dot_general(a, b, dims, preferred_element_type=F32, precision=precision)


def upright(x):
    return jnp.sum(jnp.where(iota((8, 8), 0) == iota((8, 8), 1), x, 0), axis=1, keepdims=True)


def split_hi_lo(x):
    hi = x.astype(BF16).astype(F32)
    return hi, x - hi


def pack_kernel(cos_hbm, sin_hbm, list_hbm, grid_hbm, sent_hbm, wet_hbm, diff_hbm, wgt_hbm,
                out_ref, cos_ref, sin_ref, list_ref, grid_ref, sent_ref, wet_ref, diff_ref, wgt_ref, sems):
    pairs = [(cos_hbm, cos_ref), (sin_hbm, sin_ref), (list_hbm, list_ref), (grid_hbm, grid_ref), (sent_hbm, sent_ref),
             (wet_hbm, wet_ref), (diff_hbm, diff_ref)]
    pairs += [(wgt_hbm.at[:, pl.ds(112 * side, 16), :], wgt_ref.at[side]) for side in range(2)]
    copies = [pltpu.make_async_copy(a, b, sems.at[i]) for i, (a, b) in enumerate(pairs)]
    for c in copies:
        c.start()
    me_lon = lax.axis_index("lon")
    turn = (iota((128, 1), 0) * me_lon) & 7
    half = math.sqrt(0.5)

    def eighth(k):
        values = (1.0, half, 0.0, -half, -1.0, -half, 0.0, half)
        out = jnp.zeros((128, 1), F32)
        for i, v in enumerate(values):
            out = jnp.where(((turn + k) & 7) == i, v, out)
        return out

    cos_t, sin_t = eighth(0), eighth(6)
    rho = iota((640, 1), 0)
    jh = (rho >= 320).astype(I32)
    rem = rho - 320 * jh
    tt = (rem * 205) >> 13
    rem = rem - 40 * tt
    j2 = (rem >= 20).astype(I32)
    source = (rem - 20 * j2) * 32 + 4 * tt + 2 * jh + j2
    order = onehot(iota((640, 640), 1) == source)
    row8, lane8 = iota((8, 128), 0), iota((8, 128), 1)
    for c in copies[:3]:
        c.wait()
    listing = jnp.zeros((8, 128), F32)
    for c in range(3):
        listing = jnp.where(lane8 == c, upright(list_ref[c]).astype(F32), listing)
    cos0, sin0 = cos_ref[...], sin_ref[...]
    cos_m = cos_t * cos0 - sin_t * sin0
    sin_m = -(sin_t * cos0 + cos_t * sin0)
    parts = []
    for g in range(4):
        parts += [cos_m[32 * g : 32 * g + 32], sin_m[32 * g : 32 * g + 32]]
    basis = jnp.concatenate(parts, axis=0).astype(BF16)
    for c in copies[3:]:
        c.wait()
    sums = mm(grid_ref[...].reshape(640, 640), basis, NT).astype(BF16)
    moved = mm(order, sums)
    low, high = moved[:320], moved[320:]
    for g in range(4):
        tile = jnp.concatenate([low[:, 64 * g : 64 * g + 64], high[:, 64 * g : 64 * g + 64]], axis=1)
        for t in range(8):
            block = jnp.concatenate([tile[40 * t : 40 * t + 40], listing], axis=0)
            out_ref[g * 8 + t, 0:ROW_EDGE, :] = block.astype(BF16)
    sent = sent_ref[...]
    spread = jnp.zeros((104, 128), F32)
    for c in range(5):
        pick = onehot((iota((104, 32), 0) == iota((104, 32), 1) + 20 * c) & (iota((104, 32), 1) < 20))
        block = jnp.concatenate([sent[:, 128 * c : 128 * c + 128], jnp.zeros((12, 128), F32)], axis=0)
        spread += mm(pick, block.astype(BF16))
    spread = spread.astype(BF16)
    wet = wet_ref[...].astype(F32)
    dif = diff_ref[...] * wet
    pad = jnp.zeros((12, 128), F32)
    blocks = []
    for side in range(2):
        base, lane0 = 512 * side, 126 * side
        edge = jnp.zeros((16, 128), F32)
        for k in range(6):
            if k < 5:
                src = grid_ref[4 * k : 4 * k + 4, :, base : base + 128].reshape(128, 128)
            else:
                hi, lo = split_hi_lo(dif[:, base : base + 128])
                src = jnp.concatenate(
                    [wet[:, base : base + 128], pad, hi, pad, lo, pad, jnp.zeros((32, 128), F32)], axis=0
                ).astype(BF16)
            r16, l16 = iota((16, 128), 0), iota((16, 128), 1)
            pick = onehot(((r16 == k) & (l16 == lane0)) | ((r16 == 8 + k) & (l16 == lane0 + 1)))
            edge += mm(pick, src, NT)
        pieces = [edge]
        for i in range(2):
            rows = jnp.zeros((8, 128), F32)
            for e in range(8):
                rows = jnp.where(row8 == e, wgt_ref[side, e].astype(F32)[14 * side + i : 14 * side + i + 1], rows)
            pieces.append(rows)
        blocks.append(jnp.concatenate(pieces, axis=0))
    for t in range(8):
        to_left = ((me_lon + 7) & 7) == t
        block = jnp.where(to_left, blocks[0], blocks[1]).astype(BF16)
        for g in range(4):
            out_ref[g * 8 + t, ROW_EDGE:ROW_SENT, :] = block
            out_ref[g * 8 + t, ROW_SENT:SLOT_ROWS, :] = spread


def rim_kernel(wet_hbm, diff_hbm, grid_hbm, up_ref, down_ref, wet_ref, diff_ref, rows_ref, sems):
    pairs = [(wet_hbm, wet_ref), (diff_hbm, diff_ref), (grid_hbm.at[0:2], rows_ref.at[0:2]),
             (grid_hbm.at[18:20], rows_ref.at[2:4])]
    copies = [pltpu.make_async_copy(a, b, sems.at[i]) for i, (a, b) in enumerate(pairs)]
    for c in copies:
        c.start()
    for c in copies:
        c.wait()
    row8 = iota((8, 640), 0)
    for n, (ref, first) in enumerate(((up_ref, 0), (down_ref, 18))):
        for i in range(2):
            r = first + i
            wet = wet_ref[r : r + 1, :].astype(F32)
            hi, lo = split_hi_lo(diff_ref[r : r + 1, :] * wet)
            extra = jnp.zeros((8, 640), F32)
            for m, x in enumerate((wet, hi, lo)):
                extra = jnp.where(row8 == m, x, extra)
            ref[i, 0:32, :] = rows_ref[2 * n + i]
            ref[i, 32:40, :] = extra.astype(BF16)


def remap_kernel(list_ref, recv_ref, wgt_ref, wet_ref, diff_ref,
                 rec_ref, tail_ref, planes_ref, up_ref, down_ref):
    me_grp, me_lon = lax.axis_index("grp"), lax.axis_index("lon")
    slot_l = me_grp * 8 + ((me_lon + 7) & 7)
    slot_r = me_grp * 8 + ((me_lon + 1) & 7)
    row8 = iota((8, 1), 0)

    def ids(k, s, centre):
        h = (k >= 3).astype(I32) + (k >= 6).astype(I32) + (k >= 9).astype(I32)
        lon = (centre + k - 3 * h + 7) & 7
        row = (s * 205) >> 10
        return h * 8 + lon, (s - 5 * row) * 20 + row

    lists = [tuple(upright(list_ref[c]) for c in range(3))]
    for slot in (slot_l, slot_r):
        rows = recv_ref[slot, 32:48, :].astype(F32)[8:16].astype(I32)
        lists.append((rows[:, 0:1], rows[:, 1:2], rows[:, 2:3]))
    pairs = [ids(k, s, me_lon + shift) for (k, s, _), shift in zip(lists, (0, 7, 1))]
    slot_id = jnp.concatenate([p[0] for p in pairs], axis=0)
    block_id = jnp.concatenate([p[1] for p in pairs], axis=0)
    in_block = jnp.where(iota((24, 104), 1) == block_id, 1.0, 0.0)
    source = jnp.zeros((24, 128), F32)
    for slot in range(32):
        pick = jnp.where(slot_id == slot, in_block, 0.0).astype(BF16)
        source += mm(pick, recv_ref[slot, ROW_SENT:SLOT_ROWS, :])
    own = source[0:8].astype(BF16)
    prod = jnp.zeros((8, 128), F32)
    for e in range(8):
        prod = jnp.where(row8 == e, mm(own, wgt_ref[e], NT), prod)
    target = lists[0][2]
    trow = (target * 205) >> 10
    place = jnp.where(iota((8, 256), 1) == (target - 5 * trow) * 32 + trow, 1.0, 0.0)
    placed = mm(place, prod, TN, lax.Precision.HIGHEST)
    received = jnp.concatenate([placed[32 * c : 32 * c + 20] for c in range(5)], axis=1)
    rec_ref[...] = received
    lane = iota((8, 128), 1)
    values, spots = [], []
    for n, (slot, lane0, col) in enumerate(((slot_l, 126, 4), (slot_r, 0, 0))):
        rows = recv_ref[slot, ROW_WGT:ROW_SENT, :].astype(F32)
        src = source[8 + 8 * n : 16 + 8 * n]
        v0 = jnp.sum(rows[0:8] * src, axis=1, keepdims=True)
        v1 = jnp.sum(rows[8:16] * src, axis=1, keepdims=True)
        values.append(jnp.where(lane == lane0, v0, 0.0) + jnp.where(lane == lane0 + 1, v1, 0.0))
        goal = lists[1 + n][2]
        grow = (goal * 205) >> 10
        spots.append(jnp.where((lane == grow) & (goal - 5 * grow == col), 1.0, 0.0))
    rec_tail = mm(jnp.concatenate(spots, axis=0), jnp.concatenate(values, axis=0), TN, lax.Precision.HIGHEST)[0:20]
    edge = jnp.concatenate(
        [recv_ref[slot_l, ROW_EDGE:ROW_WGT, :].astype(F32), recv_ref[slot_r, ROW_EDGE:ROW_WGT, :].astype(F32)], axis=0
    ).astype(BF16)
    r32, l32 = iota((32, 128), 0), iota((32, 128), 1)

    def tail_of(k):
        pick = onehot(
            ((r32 == k) & (l32 == 126)) | ((r32 == 8 + k) & (l32 == 127))
            | ((r32 == 16 + k) & (l32 == 0)) | ((r32 == 24 + k) & (l32 == 1))
        )
        return mm(edge, pick, TN)

    for k in range(5):
        tail_ref[4 * k : 4 * k + 4] = tail_of(k).reshape(4, 32, 128).astype(BF16)
    last = tail_of(5)
    own_wet = wet_ref[...].astype(F32)
    wet = jnp.concatenate([own_wet, last[0:20]], axis=1)
    dif = jnp.concatenate([diff_ref[...] * own_wet, last[32:52] + last[64:84]], axis=1)
    force = wet * jnp.concatenate([received, rec_tail], axis=1)
    planes_ref[0] = wet
    planes_ref[1] = dif
    planes_ref[2] = force
    fhi, flo = split_hi_lo(force)
    row16 = iota((16, 128), 0)
    for ref, first in ((up_ref, 0), (down_ref, 18)):
        for i in range(2):
            r = first + i
            ref[i, 0:32, :] = tail_ref[r]
            extra = jnp.zeros((16, 128), F32)
            lines = [x[r : r + 1, 128 * c : 128 * c + 128] for x in (fhi, flo) for c in range(6)]
            lines += [last[r : r + 1], last[32 + r : 33 + r], last[64 + r : 65 + r]]
            for m, x in enumerate(lines):
                extra = jnp.where(row16 == m, x, extra)
            ref[i, 32:48, :] = extra.astype(BF16)


def step_kernel(tail_ref, planes_ref, above_ref, below_ref, above2_ref, below2_ref, grid_ref,
                out_hbm, q_ref, u_ref, q1_ref, u1_ref, wet_ref, dif_ref, c_ref, res_ref, sems):
    level0 = iota((8, WIDE), 0) == 0

    def load(r, row, end, wet, dif, force):
        wet = jnp.broadcast_to(wet, (8, WIDE))
        wet_ref[r] = wet
        dif_ref[r] = jnp.broadcast_to(dif, (8, WIDE))
        cells = jnp.concatenate([row.astype(F32), end.astype(F32)], axis=1)
        for v in range(4):
            part = cells[8 * v : 8 * v + 8]
            if v == 0:
                part = jnp.where(level0, part + force, part)
            q_ref[r, 8 * v : 8 * v + 8, :] = part
            u_ref[r, 8 * v : 8 * v + 8, :] = part * wet

    for ref, ref2, base in ((above_ref, above2_ref, 0), (below_ref, below2_ref, 22)):
        for i in range(2):
            near = ref[i, 32:40, :].astype(F32)
            far = ref2[i, 32:48, :].astype(F32)
            wet = jnp.concatenate([near[0:1], far[12:13]], axis=1)
            dif = jnp.concatenate([near[1:2] + near[2:3], far[13:14] + far[14:15]], axis=1)
            force = jnp.concatenate([far[c : c + 1] + far[6 + c : 7 + c] for c in range(6)], axis=1)
            load(base + i, ref[i, 0:32, :], ref2[i, 0:32, :], wet, dif, force)
    for r in range(20):
        load(r + 2, grid_ref[r], tail_ref[r], planes_ref[0, r : r + 1, :], planes_ref[1, r : r + 1, :],
             planes_ref[2, r : r + 1, :])

    def sides(x):
        return pltpu.roll(x, 1, axis=1) + pltpu.roll(x, WIDE - 1, axis=1)

    def first(r, carry):
        dif = dif_ref[r]
        wet = wet_ref[r]
        coef = 1.0 - dif * (wet_ref[r - 1] + wet_ref[r + 1] + sides(wet))
        c_ref[r] = coef
        for v in range(4):
            lev = pl.ds(8 * v, 8)
            total = sides(u_ref[r, lev, :]) + u_ref[r - 1, lev, :] + u_ref[r + 1, lev, :]
            q = q_ref[r, lev, :] * coef + dif * total
            q1_ref[r, lev, :] = q
            u1_ref[r, lev, :] = q * wet
        return carry

    lax.fori_loop(1, 23, first, 0)

    def copy(r):
        return pltpu.make_async_copy(res_ref.at[r], out_hbm.at[r], sems.at[r])

    def second(r, carry):
        coef = c_ref[r]
        dif = dif_ref[r]
        for v in range(4):
            lev = pl.ds(8 * v, 8)
            total = sides(u1_ref[r, lev, :]) + u1_ref[r - 1, lev, :] + u1_ref[r + 1, lev, :]
            q = q1_ref[r, lev, :] * coef + dif * total
            res_ref[r - 2, lev, :] = q[:, 0:640]
        copy(r - 2).start()
        return carry

    lax.fori_loop(2, 22, second, 0)

    def finish(r, carry):
        copy(r).wait()
        return carry

    lax.fori_loop(0, 20, finish, 0)


def turn_kernel(recv_ref, out_ref):
    norm = np.float32(1.0 / math.sqrt(5120.0))
    sums = []
    for g in range(3):
        acc = recv_ref[g * 8, 0:48, :].astype(F32)
        for t in range(1, 8):
            acc += recv_ref[g * 8 + t, 0:48, :].astype(F32)
        sums.append(acc[0:40])
    stack = (jnp.concatenate(sums + [jnp.zeros((8, 128), F32)], axis=0) * norm).astype(BF16)
    out = jnp.zeros((256, 128), F32)
    for j2 in range(2):
        lane = iota((128, 128), 0)
        g = (lane >= 20).astype(I32) + (lane >= 40).astype(I32)
        pick = onehot((iota((128, 128), 1) == lane + 20 * g + 20 * j2) & (lane < 60))
        lined = mm(pick, stack).astype(BF16)
        rho, lam = iota((256, 128), 0), iota((256, 128), 1)
        want = ((rho >> 2) & 1) * 64 + (rho & 1) * 32 + (rho >> 3)
        place = onehot((((rho >> 1) & 1) == j2) & (lam == want))
        out += mm(place, lined, NT)
    out_ref[...] = out.astype(BF16)


def legendre_kernel(waves_hbm, table_hbm, after_hbm, out_ref, waves_ref, table_ref, sems):
    copies = [
        pltpu.make_async_copy(table_hbm.at[pl.ds(128 * i, 128), :], table_ref.at[pl.ds(128 * i, 128), :], sems.at[i])
        for i in range(15)
    ]
    first = pltpu.make_async_copy(waves_hbm, waves_ref, sems.at[15])
    first.start()
    for c in copies:
        c.start()
    first.wait()
    lane = iota((8, 128), 1)
    waves = [waves_ref[l].astype(F32) for l in range(32)]
    tiles = []
    for tau in range(15):
        tile = jnp.zeros((8, 128), F32)
        for g in range(3):
            for l in range(32):
                start = g * 640 + l * 20 - 128 * tau
                if start <= -20 or start >= 128:
                    continue
                shift = (start - 20 * g) % 128
                moved = pltpu.roll(waves[l], shift, axis=1) if shift else waves[l]
                tile = jnp.where((lane >= start) & (lane < start + 20), moved, tile)
        tiles.append(tile)
    out = jnp.zeros((8, 1280), F32)
    for i in range(15):
        copies[i].wait()
        out += mm(tiles[i].astype(BF16), table_ref[128 * i : 128 * i + 128, :])
    for j in range(4):
        out_ref[j] = out[2 * j : 2 * j + 2]


VMEM = pl.BlockSpec(memory_space=pltpu.VMEM)
SMEM = pl.BlockSpec(memory_space=pltpu.SMEM)
HBM = pl.BlockSpec(memory_space=pltpu.HBM)


def call(kernel, name, smem, vmem, hbm, outs, scratch=(), out_space=VMEM, limit=None):
    flat = [jax.ShapeDtypeStruct(s, d) for s, d in outs]
    return pl.pallas_call(
        kernel,
        name=name,
        out_shape=flat if len(flat) > 1 else flat[0],
        in_specs=[SMEM] * len(smem) + [VMEM] * len(vmem) + [HBM] * len(hbm),
        out_specs=[out_space] * len(flat) if len(flat) > 1 else out_space,
        scratch_shapes=list(scratch),
        compiler_params=pltpu.CompilerParams(vmem_limit_bytes=limit and limit * 1024 * 1024),
    )(*smem, *vmem, *hbm)


def trig_tables():
    phase = np.arange(128)[:, None] * np.arange(640)[None, :] % 5120
    angle = 2.0 * np.pi / 5120.0 * phase
    return np.cos(angle).astype(np.float32), np.sin(angle).astype(np.float32)


def shards(grid_state, legendre, sent_field, wet_mask, diffusivity, remap_blocks, remap_weights):
    rows = grid_state.transpose(1, 0, 2)
    listing = remap_blocks.transpose(0, 3, 1, 2).reshape(3, 1, 8)
    weights = remap_weights[0, 0]
    bands = lax.axis_size(("grp", "lat"))
    to_before = [((i + 1) % bands, i) for i in range(bands)]
    to_after = [(i, (i + 1) % bands) for i in range(bands)]
    cos0, sin0 = trig_tables()
    packed = call(
        pack_kernel, "pack", (), (),
        (jnp.asarray(cos0), jnp.asarray(sin0), listing, rows, sent_field, wet_mask, diffusivity, weights),
        [((32, SLOT_ROWS, 128), BF16)],
        scratch=[pltpu.VMEM((128, 640), F32), pltpu.VMEM((128, 640), F32), pltpu.VMEM((3, 1, 8), I32), pltpu.VMEM((20, 32, 640), BF16),
                 pltpu.VMEM((20, 640), F32), pltpu.VMEM((20, 640), I32), pltpu.VMEM((20, 640), F32),
                 pltpu.VMEM((2, 8, 16, 128), BF16), pltpu.SemaphoreType.DMA((9,))],
    )
    plane = lax.all_to_all(packed, ("grp", "lon"), 0, 0, tiled=True)
    up, down = call(
        rim_kernel, "rim", (), (), (wet_mask, diffusivity, rows),
        [((2, 40, 640), BF16), ((2, 40, 640), BF16)],
        scratch=[pltpu.VMEM((20, 640), I32), pltpu.VMEM((20, 640), F32), pltpu.VMEM((4, 32, 640), BF16),
                 pltpu.SemaphoreType.DMA((4,))],
    )
    below = lax.ppermute(up, ("grp", "lat"), to_before)
    above = lax.ppermute(down, ("grp", "lat"), to_after)
    plane, above, below = lax.optimization_barrier((plane, above, below))
    turned = call(turn_kernel, "turn", (), (plane,), (), [((256, 128), BF16)], limit=16)
    waves = lax.all_to_all(turned.reshape(32, 8, 128), "lat", 0, 0, tiled=True)
    received, tail, planes, up2, down2 = call(
        remap_kernel, "remap", (), (listing, plane, weights, wet_mask, diffusivity), (),
        [((20, 640), F32), ((20, 32, 128), BF16), ((3, 20, WIDE), F32), ((2, 48, 128), BF16), ((2, 48, 128), BF16)],
        limit=16,
    )
    below2 = lax.ppermute(up2, ("grp", "lat"), to_before)
    above2 = lax.ppermute(down2, ("grp", "lat"), to_after)
    stepped = call(
        step_kernel, "step", (), (tail, planes, above, below, above2, below2, rows), (),
        [((20, 32, 640), F32)],
        scratch=[pltpu.VMEM((24, 32, WIDE), F32)] * 4 + [pltpu.VMEM((24, 8, WIDE), F32)] * 3
        + [pltpu.VMEM((20, 32, 640), F32), pltpu.SemaphoreType.DMA((20,))],
        out_space=HBM, limit=32,
    )
    spectral = call(
        legendre_kernel, "legendre", (), (), (waves, legendre[0], stepped), [((4, 2, 1280), F32)],
        scratch=[pltpu.VMEM((32, 8, 128), BF16), pltpu.VMEM((1920, 1280), BF16), pltpu.SemaphoreType.DMA((16,))],
    )
    return spectral.reshape(1, 4, 2, 1280), received, stepped.transpose(1, 0, 2)


def solution(mesh):
    in_specs = (
        P(None, ("grp", "lat"), "lon"),
        P(("grp", "lat"), None, None),
        P(("grp", "lat"), "lon"),
        P(("grp", "lat"), "lon"),
        P(("grp", "lat"), "lon"),
        P(("grp", "lat"), "lon", None, None),
        P(("grp", "lat"), "lon", None, None, None),
    )
    out_specs = (
        P(("grp", "lat"), "lon", None, None),
        P(("grp", "lat"), "lon"),
        P(None, ("grp", "lat"), "lon"),
    )
    return jax.shard_map(shards, mesh=mesh, in_specs=in_specs, out_specs=out_specs, check_vma=False)
```

time: 100 us -> 94.4 us (0.944)
  blocking collectives: 39.3 us -> 0 us
  starting transfers between devices: 26.8 us -> 55.1 us
  waiting for transfers between devices: 6.51 us -> 18.4 us
  local copies, waits for them, and re-layouts: 8.79 us -> 0.65 us
  Pallas kernels: 14.5 us -> 18.9 us
  matrix products: 3.18 us -> 0 us
    all_to_all x1 -> x0, blocking collectives: 39.3 us -> none  [shards(): plane = lax.all_to_all(packed, ('grp', 'lon'), 0, 0, tiled=True)]
    all_to_all x0 -> x1, starting transfers between devices: none -> 17.8 us  [shards(): plane = lax.all_to_all(packed, ('grp', 'lon'), 0, 0, tiled=True)]
    ppermute x2 -> x4, starting transfers between devices: 6.76 us -> 18.1 us  [the longest x1 9.45 us: shards(): below = lax.ppermute(up, ('grp', 'lat'), to_before)]
    unnamed x25 -> x12, local copies, waits for them, and re-layouts: 8.12 us -> 0.65 us
    all_to_all x0 -> x1, waiting for transfers between devices: none -> 7.34 us  [shards(): plane = lax.all_to_all(packed, ('grp', 'lon'), 0, 0, tiled=True)]
    all_to_all x1, waiting for transfers between devices: 3.23 us -> 7.7 us  [shards(): waves = lax.all_to_all(turned.reshape(32, 8, 128), 'lat', 0, 0, tiled=True)]
    pallas_call x4 -> x6, Pallas kernels: 14.5 us -> 18.9 us  [call(): pl.pallas_call(kernel, name=name, out_shape=flat if len(flat) > 1 else fl...]
    dot_general x1 -> x0, matrix products: 3.18 us -> none  [mm(): lax.dot_general(a, b, dims, preferred_element_type=F32, precision=precision)]
  transfers between devices with their start and end apart: 3 -> 6, of which waited for: 2 -> 5; matrix products, arithmetic and copies ran while one was open for 0% -> 0% of each run, Pallas kernels for 11% -> 11%
where the time goes in v2:
time: 94.4 us; the launch traced here: 94 us
  starting transfers between devices  55.1 us (58%)
  Pallas kernels  18.9 us (20%)
  waiting for transfers between devices  18.4 us (19%)
    all_to_all x1, starting transfers between devices, shards(): waves = lax.all_to_all(turned.reshape(32, 8, 128), 'lat', 0, 0, tiled=True)  19.2 us
    pallas_call x6, Pallas kernels, call(): pl.pallas_call(kernel, name=name, out_shape=flat if len(flat) > 1 else fl...  18.9 us
    all_to_all x1, starting transfers between devices, shards(): plane = lax.all_to_all(packed, ('grp', 'lon'), 0, 0, tiled=True)  17.8 us
    ppermute x1, starting transfers between devices, shards(): below = lax.ppermute(up, ('grp', 'lat'), to_before)  9.45 us
    all_to_all x1, waiting for transfers between devices, shards(): waves = lax.all_to_all(turned.reshape(32, 8, 128), 'lat', 0, 0, tiled=True)  7.7 us
    all_to_all x1, waiting for transfers between devices, shards(): plane = lax.all_to_all(packed, ('grp', 'lon'), 0, 0, tiled=True)  7.34 us
    ppermute x1, starting transfers between devices, shards(): below2 = lax.ppermute(up2, ('grp', 'lat'), to_before)  3.64 us
    ppermute x1, starting transfers between devices, shards(): above2 = lax.ppermute(down2, ('grp', 'lat'), to_after)  3.13 us
  transfers between devices with their start and end apart: 6, of which 5 were waited for; matrix products, arithmetic and copies ran while one was open for 0% of the time, Pallas kernels for 11%

profile of v2, /device:TPU:1, one launch (start us, length us, event | category | flops | bytes accessed | tf_op | source)
XLA Modules:
  0.0 94.0 jit_solution(15921222314293838741)
XLA Ops:
  0.6 4.1 %pack.1 = bf16[32,184,128]{2,1,0:T(8,128)(2,1)} custom-call(f32[128,640]{1,0:T(8,128)} %constant.4.clone.cos_hbm, f32[128,640]{1,0:T(8,128)} %constant.5.clone.sin_hbm, s32[3,1,8]{2,1,0:T(1,128)} %bitcast.14, bf16[20,32,640]{2,1,0:T(8,128)(2,1)} %bitcast.9, f32[20,640]{1,0:T(8,128)} %sent_hbm.1, s32[20,640]{1,0:T(8,128)} %wet_ref.1, f32[20,640]{1,0:T(8,128)} %diff_ref.1, ...), custom_call_target="tpu_custom_call" | custom-call | tf_op jit(solution)/shard_map/pack/pallas_call | solution.py:371
  4.7 17.8 %all-to-all-start = ((bf16[32,184,128]{2,1,0:T(8,128)(2,1)}), bf16[32,184,128]{2,1,0:T(8,128)(2,1)S(1)}, u32[]{:S(2)}, u32[]{:S(2)}) async-start(bf16[32,184,128]{2,1,0:T(8,128)(2,1)} %pack.1), calls=%async_computation | async-start | bytes 3014656 | tf_op jit(solution)/shard_map/all_to_all | solution.py:404
  22.5 0.0 copy-start.1
  22.5 0.0 copy-start.2
  22.5 0.0 copy-start.3
  22.5 0.0 copy-start.4
  22.5 1.8 %rim.1 = (bf16[2,40,640]{2,1,0:T(8,128)(2,1)}, bf16[2,40,640]{2,1,0:T(8,128)(2,1)}) custom-call(s32[20,640]{1,0:T(8,128)} %wet_ref.1, f32[20,640]{1,0:T(8,128)} %diff_ref.1, bf16[20,32,640]{2,1,0:T(8,128)(2,1)} %bitcast.10), custom_call_target="tpu_custom_call" | custom-call | tf_op jit(solution)/shard_map/rim/pallas_call | solution.py:371
  24.3 1.9 %collective-permute-start = (bf16[2,40,640]{2,1,0:T(8,128)(2,1)}, bf16[2,40,640]{2,1,0:T(8,128)(2,1)S(1)}, u32[]{:S(2)}, u32[]{:S(2)}) collective-permute-start(bf16[2,40,640]{2,1,0:T(8,128)(2,1)} %get-tuple-element.13), channel_id=1, source_target_pairs={{0,8},{8,16},{16,24},{24,32},{32,40},{40,48},{48,56},{56,64},{64,7... | collective-permute-start | bytes 307208 | tf_op jit(solution)/shard_map/ppermute | solution.py:412
  26.3 0.0 copy-start
  26.3 9.4 %collective-permute-start.1 = (bf16[2,40,640]{2,1,0:T(8,128)(2,1)}, bf16[2,40,640]{2,1,0:T(8,128)(2,1)S(1)}, u32[]{:S(2)}, u32[]{:S(2)}) collective-permute-start(bf16[2,40,640]{2,1,0:T(8,128)(2,1)} %get-tuple-element.14), channel_id=1, source_target_pairs={{8,0},{16,8},{24,16},{32,24},{40,32},{48,40},{56,48},{64,56},{72,6... | collective-permute-start | bytes 307208 | tf_op jit(solution)/shard_map/ppermute | solution.py:411
  35.7 1.4 %collective-permute-done.above_ref = bf16[2,40,640]{2,1,0:T(8,128)(2,1)S(1)} collective-permute-done((bf16[2,40,640]{2,1,0:T(8,128)(2,1)}, bf16[2,40,640]{2,1,0:T(8,128)(2,1)S(1)}, u32[]{:S(2)}, u32[]{:S(2)}) %collective-permute-start) | collective-permute-done | bytes 102432 | tf_op jit(solution)/shard_map/ppermute | solution.py:412
  37.2 0.5 collective-permute-done.1.below_ref
  37.7 7.3 %all-to-all-done.recv_ref = bf16[32,184,128]{2,1,0:T(8,128)(2,1)S(1)} async-done(((bf16[32,184,128]{2,1,0:T(8,128)(2,1)}), bf16[32,184,128]{2,1,0:T(8,128)(2,1)S(1)}, u32[]{:S(2)}, u32[]{:S(2)}) %all-to-all-start) | async-done | bytes 1507360 | tf_op jit(solution)/shard_map/all_to_all | solution.py:404
  45.0 1.0 %turn.1 = bf16[256,128]{1,0:T(8,128)(2,1)} custom-call(bf16[32,184,128]{2,1,0:T(8,128)(2,1)S(1)} %all-to-all-done.recv_ref), custom_call_target="tpu_custom_call" | custom-call | tf_op jit(solution)/shard_map/turn/pallas_call | solution.py:371
  46.0 19.2 %all-to-all-start.1 = ((bf16[32,8,128]{2,1,0:T(8,128)(2,1)}), bf16[32,8,128]{2,1,0:T(8,128)(2,1)S(1)}, u32[]{:S(2)}, u32[]{:S(2)}) async-start(bf16[32,8,128]{2,1,0:T(8,128)(2,1)} %bitcast.4), calls=%async_computation.1 | async-start | bytes 131072 | tf_op jit(solution)/shard_map/all_to_all | solution.py:415
  65.2 0.0 copy-done.1
  65.2 0.0 copy-done.2
  65.3 0.0 copy-done.3
  65.3 0.0 copy-done.4
  65.3 2.1 %remap.1 = (f32[20,640]{1,0:T(8,128)}, bf16[20,32,128]{2,1,0:T(8,128)(2,1)S(1)}, f32[3,20,768]{2,1,0:T(8,128)S(1)}, bf16[2,48,128]{2,1,0:T(8,128)(2,1)S(1)}, bf16[2,48,128]{2,1,0:T(8,128)(2,1)S(1)}) custom-call(s32[3,1,8]{2,1,0:T(1,128)S(1)} %bitcast.15, bf16[32,184,128]{2,1,0:T(8,128)(2,1)S(1)} %all-to-all-done.recv_ref, bf16[8,128,128]{2,1,0:T(8,128)(2,1)S(1)} %bitcast.13, ...), custom_call_target="tpu_custom_call" | custom-call | tf_op jit(solution)/shard_map/remap/pallas_call | solution.py:371
  67.3 3.1 %collective-permute-start.2 = (bf16[2,48,128]{2,1,0:T(8,128)(2,1)S(1)}, bf16[2,48,128]{2,1,0:T(8,128)(2,1)S(1)}, u32[]{:S(2)}, u32[]{:S(2)}) collective-permute-start(bf16[2,48,128]{2,1,0:T(8,128)(2,1)S(1)} %get-tuple-element.20), channel_id=1, source_target_pairs={{0,8},{8,16},{16,24},{24,32},{32,40},{40,48},{48,56},{56,64},{64,7... | collective-permute-start | bytes 73736 | tf_op jit(solution)/shard_map/ppermute | solution.py:422
  70.5 3.6 %collective-permute-start.3 = (bf16[2,48,128]{2,1,0:T(8,128)(2,1)S(1)}, bf16[2,48,128]{2,1,0:T(8,128)(2,1)S(1)}, u32[]{:S(2)}, u32[]{:S(2)}) collective-permute-start(bf16[2,48,128]{2,1,0:T(8,128)(2,1)S(1)} %get-tuple-element.21), channel_id=1, source_target_pairs={{8,0},{16,8},{24,16},{32,24},{40,32},{48,40},{56,48},{64,56},{72,6... | collective-permute-start | bytes 73736 | tf_op jit(solution)/shard_map/ppermute | solution.py:421
  74.1 0.0 collective-permute-done.2.above2_ref
  74.1 1.4 %collective-permute-done.3.below2_ref = bf16[2,48,128]{2,1,0:T(8,128)(2,1)S(1)} collective-permute-done((bf16[2,48,128]{2,1,0:T(8,128)(2,1)S(1)}, bf16[2,48,128]{2,1,0:T(8,128)(2,1)S(1)}, u32[]{:S(2)}, u32[]{:S(2)}) %collective-permute-start.3) | collective-permute-done | bytes 24608 | tf_op jit(solution)/shard_map/ppermute | solution.py:421
  75.6 0.0 copy-done
  75.6 6.8 %step.1.after_hbm = f32[20,32,640]{2,1,0:T(8,128)} custom-call(bf16[20,32,128]{2,1,0:T(8,128)(2,1)S(1)} %get-tuple-element.16.tail_ref, f32[3,20,768]{2,1,0:T(8,128)S(1)} %get-tuple-element.17.planes_ref, bf16[2,40,640]{2,1,0:T(8,128)(2,1)S(1)} %collective-permute-done.above_ref, bf16[2,40,640]{2,1,0:T(8,128)(2,1)S(1)} %collective-permute-done.1.below_ref, ...), custom_call_target="tpu_custom_call" | custom-call | tf_op jit(solution)/shard_map/step/pallas_call | solution.py:371
  82.3 7.7 %all-to-all-done.1.waves_hbm = bf16[32,8,128]{2,1,0:T(8,128)(2,1)S(1)} async-done(((bf16[32,8,128]{2,1,0:T(8,128)(2,1)}), bf16[32,8,128]{2,1,0:T(8,128)(2,1)S(1)}, u32[]{:S(2)}, u32[]{:S(2)}) %all-to-all-start.1) | async-done | bytes 65568 | tf_op jit(solution)/shard_map/all_to_all | solution.py:415
  90.0 0.0 copy-start.5
  90.0 0.6 copy-done.5
  90.6 3.3 %legendre.1 = f32[4,2,1280]{2,1,0:T(2,128)} custom-call(bf16[32,8,128]{2,1,0:T(8,128)(2,1)} %copy-done.5, bf16[1920,1280]{1,0:T(8,128)(2,1)} %bitcast.17, f32[20,32,640]{2,1,0:T(8,128)} %step.1.after_hbm), custom_call_target="tpu_custom_call" | custom-call | tf_op jit(solution)/shard_map/legendre/pallas_call | solution.py:371
Async XLA Ops:
  4.7 40.3 %all-to-all-start = ((bf16[32,184,128]{2,1,0:T(8,128)(2,1)}), bf16[32,184,128]{2,1,0:T(8,128)(2,1)S(1)}, u32[]{:S(2)}, u32[]{:S(2)}) async-start(bf16[32,184,128]{2,1,0:T(8,128)(2,1)} %pack.1), calls=%async_computation | async-start | bytes 3014656 | tf_op jit(solution)/shard_map/all_to_all | solution.py:404
  22.5 42.7 %copy-start.1 = (bf16[1,1,8,128,128]{4,3,2,1,0:T(8,128)(2,1)S(1)}, bf16[1,1,8,128,128]{4,3,2,1,0:T(8,128)(2,1)}, u32[]{:S(2)}) copy-start(bf16[1,1,8,128,128]{4,3,2,1,0:T(8,128)(2,1)} %param.15) | copy-start | bytes 786436
  22.5 42.7 %copy-start.2 = (s32[20,640]{1,0:T(8,128)S(1)}, s32[20,640]{1,0:T(8,128)}, u32[]{:S(2)}) copy-start(s32[20,640]{1,0:T(8,128)} %wet_ref.1) | copy-start | bytes 153604
  22.5 42.7 %copy-start.3 = (f32[20,640]{1,0:T(8,128)S(1)}, f32[20,640]{1,0:T(8,128)}, u32[]{:S(2)}) copy-start(f32[20,640]{1,0:T(8,128)} %diff_ref.1) | copy-start | bytes 153604
  22.5 42.7 %copy-start.4 = (s32[1,1,8,3]{2,1,3,0:T(1,128)S(1)}, s32[1,1,8,3]{2,1,3,0:T(1,128)}, u32[]{:S(2)}) copy-start(s32[1,1,8,3]{2,1,3,0:T(1,128)} %param.14) | copy-start | bytes 292
  24.3 12.8 %collective-permute-start = (bf16[2,40,640]{2,1,0:T(8,128)(2,1)}, bf16[2,40,640]{2,1,0:T(8,128)(2,1)S(1)}, u32[]{:S(2)}, u32[]{:S(2)}) collective-permute-start(bf16[2,40,640]{2,1,0:T(8,128)(2,1)} %get-tuple-element.13), channel_id=1, source_target_pairs={{0,8},{8,16},{16,24},{24,32},{32,40},{40,48},{48,56},{56,64},{64,7... | collective-permute-start | bytes 307208 | tf_op jit(solution)/shard_map/ppermute | solution.py:412
  26.3 49.3 %copy-start = (bf16[32,20,640]{2,0,1:T(8,128)(2,1)S(1)}, bf16[32,20,640]{2,0,1:T(8,128)(2,1)}, u32[]{:S(2)}) copy-start(bf16[32,20,640]{2,0,1:T(8,128)(2,1)} %param.9) | copy-start | bytes 2457604
  26.3 11.4 %collective-permute-start.1 = (bf16[2,40,640]{2,1,0:T(8,128)(2,1)}, bf16[2,40,640]{2,1,0:T(8,128)(2,1)S(1)}, u32[]{:S(2)}, u32[]{:S(2)}) collective-permute-start(bf16[2,40,640]{2,1,0:T(8,128)(2,1)} %get-tuple-element.14), channel_id=1, source_target_pairs={{8,0},{16,8},{24,16},{32,24},{40,32},{48,40},{56,48},{64,56},{72,6... | collective-permute-start | bytes 307208 | tf_op jit(solution)/shard_map/ppermute | solution.py:411
  46.0 44.0 %all-to-all-start.1 = ((bf16[32,8,128]{2,1,0:T(8,128)(2,1)}), bf16[32,8,128]{2,1,0:T(8,128)(2,1)S(1)}, u32[]{:S(2)}, u32[]{:S(2)}) async-start(bf16[32,8,128]{2,1,0:T(8,128)(2,1)} %bitcast.4), calls=%async_computation.1 | async-start | bytes 131072 | tf_op jit(solution)/shard_map/all_to_all | solution.py:415
  67.3 6.8 %collective-permute-start.2 = (bf16[2,48,128]{2,1,0:T(8,128)(2,1)S(1)}, bf16[2,48,128]{2,1,0:T(8,128)(2,1)S(1)}, u32[]{:S(2)}, u32[]{:S(2)}) collective-permute-start(bf16[2,48,128]{2,1,0:T(8,128)(2,1)S(1)} %get-tuple-element.20), channel_id=1, source_target_pairs={{0,8},{8,16},{16,24},{24,32},{32,40},{40,48},{48,56},{56,64},{64,7... | collective-permute-start | bytes 73736 | tf_op jit(solution)/shard_map/ppermute | solution.py:422
  70.5 5.1 %collective-permute-start.3 = (bf16[2,48,128]{2,1,0:T(8,128)(2,1)S(1)}, bf16[2,48,128]{2,1,0:T(8,128)(2,1)S(1)}, u32[]{:S(2)}, u32[]{:S(2)}) collective-permute-start(bf16[2,48,128]{2,1,0:T(8,128)(2,1)S(1)} %get-tuple-element.21), channel_id=1, source_target_pairs={{8,0},{16,8},{24,16},{32,24},{40,32},{48,40},{56,48},{64,56},{72,6... | collective-permute-start | bytes 73736 | tf_op jit(solution)/shard_map/ppermute | solution.py:421
  90.0 0.6 copy-start.5

commit v3 on v2

--- a/solution.py
+++ b/solution.py
@@ -16,10 +16,10 @@
 TN = (((0,), (0,)), ((), ()))
 
 WIDE = 768
-ROW_EDGE = 48
-ROW_WGT = 64
-ROW_SENT = 80
-SLOT_ROWS = 184
+ROW_WGT = 16
+ROW_LIST = 32
+AREA = 104
+SLOT_ROWS = 144
 
 
 def iota(shape, dim):
@@ -45,9 +45,9 @@
 
 def pack_kernel(cos_hbm, sin_hbm, list_hbm, grid_hbm, sent_hbm, wet_hbm, diff_hbm, wgt_hbm,
                 out_ref, cos_ref, sin_ref, list_ref, grid_ref, sent_ref, wet_ref, diff_ref, wgt_ref, sems):
-    pairs = [(cos_hbm, cos_ref), (sin_hbm, sin_ref), (list_hbm, list_ref), (grid_hbm, grid_ref), (sent_hbm, sent_ref),
-             (wet_hbm, wet_ref), (diff_hbm, diff_ref)]
+    pairs = [(list_hbm, list_ref), (sent_hbm, sent_ref), (wet_hbm, wet_ref), (diff_hbm, diff_ref)]
     pairs += [(wgt_hbm.at[:, pl.ds(112 * side, 16), :], wgt_ref.at[side]) for side in range(2)]
+    pairs += [(cos_hbm, cos_ref), (sin_hbm, sin_ref), (grid_hbm, grid_ref)]
     copies = [pltpu.make_async_copy(a, b, sems.at[i]) for i, (a, b) in enumerate(pairs)]
     for c in copies:
         c.start()
@@ -72,11 +72,34 @@
     source = (rem - 20 * j2) * 32 + 4 * tt + 2 * jh + j2
     order = onehot(iota((640, 640), 1) == source)
     row8, lane8 = iota((8, 128), 0), iota((8, 128), 1)
-    for c in copies[:3]:
+    for c in copies[:6]:
         c.wait()
     listing = jnp.zeros((8, 128), F32)
     for c in range(3):
         listing = jnp.where(lane8 == c, upright(list_ref[c]).astype(F32), listing)
+    sent = sent_ref[...]
+    spread = jnp.zeros((104, 128), F32)
+    for c in range(5):
+        pick = onehot((iota((104, 32), 0) == iota((104, 32), 1) + 20 * c) & (iota((104, 32), 1) < 20))
+        block = jnp.concatenate([sent[:, 128 * c : 128 * c + 128], jnp.zeros((12, 128), F32)], axis=0)
+        spread += mm(pick, block.astype(BF16))
+    wet = wet_ref[...].astype(F32)
+    dif = diff_ref[...] * wet
+    pad = jnp.zeros((12, 128), F32)
+    wgt, planes = [], []
+    for side in range(2):
+        base = 512 * side
+        hi, lo = split_hi_lo(dif[:, base : base + 128])
+        planes.append(jnp.concatenate(
+            [wet[:, base : base + 128], pad, hi, pad, lo, pad, jnp.zeros((32, 128), F32)], axis=0
+        ).astype(BF16))
+        for i in range(2):
+            rows = jnp.zeros((8, 128), F32)
+            for e in range(8):
+                rows = jnp.where(row8 == e, wgt_ref[side, e].astype(F32)[14 * side + i : 14 * side + i + 1], rows)
+            wgt.append(rows)
+    for c in copies[6:8]:
+        c.wait()
     cos0, sin0 = cos_ref[...], sin_ref[...]
     cos_m = cos_t * cos0 - sin_t * sin0
     sin_m = -(sin_t * cos0 + cos_t * sin0)
@@ -84,54 +107,32 @@
     for g in range(4):
         parts += [cos_m[32 * g : 32 * g + 32], sin_m[32 * g : 32 * g + 32]]
     basis = jnp.concatenate(parts, axis=0).astype(BF16)
-    for c in copies[3:]:
-        c.wait()
+    copies[8].wait()
     sums = mm(grid_ref[...].reshape(640, 640), basis, NT).astype(BF16)
+    blocks = []
+    for side in range(2):
+        base, lane0 = 512 * side, 126 * side
+        edge = jnp.zeros((16, 128), F32)
+        for k in range(6):
+            src = grid_ref[4 * k : 4 * k + 4, :, base : base + 128].reshape(128, 128) if k < 5 else planes[side]
+            r16, l16 = iota((16, 128), 0), iota((16, 128), 1)
+            pick = onehot(((r16 == k) & (l16 == lane0)) | ((r16 == 8 + k) & (l16 == lane0 + 1)))
+            edge += mm(pick, src, NT)
+        pieces = [edge, wgt[2 * side], wgt[2 * side + 1], listing, jnp.zeros((AREA - 40, 128), F32)]
+        blocks.append(jnp.concatenate(pieces, axis=0))
+    for g in range(4):
+        same = lax.axis_index("grp") == g
+        left = jnp.where(same, blocks[0], spread)
+        right = jnp.where(same, blocks[1], spread)
+        for t in range(8):
+            to_left = ((me_lon + 7) & 7) == t
+            out_ref[g * 8 + t, 0:AREA, :] = jnp.where(to_left, left, right).astype(BF16)
     moved = mm(order, sums)
     low, high = moved[:320], moved[320:]
     for g in range(4):
         tile = jnp.concatenate([low[:, 64 * g : 64 * g + 64], high[:, 64 * g : 64 * g + 64]], axis=1)
         for t in range(8):
-            block = jnp.concatenate([tile[40 * t : 40 * t + 40], listing], axis=0)
-            out_ref[g * 8 + t, 0:ROW_EDGE, :] = block.astype(BF16)
-    sent = sent_ref[...]
-    spread = jnp.zeros((104, 128), F32)
-    for c in range(5):
-        pick = onehot((iota((104, 32), 0) == iota((104, 32), 1) + 20 * c) & (iota((104, 32), 1) < 20))
-        block = jnp.concatenate([sent[:, 128 * c : 128 * c + 128], jnp.zeros((12, 128), F32)], axis=0)
-        spread += mm(pick, block.astype(BF16))
-    spread = spread.astype(BF16)
-    wet = wet_ref[...].astype(F32)
-    dif = diff_ref[...] * wet
-    pad = jnp.zeros((12, 128), F32)
-    blocks = []
-    for side in range(2):
-        base, lane0 = 512 * side, 126 * side
-        edge = jnp.zeros((16, 128), F32)
-        for k in range(6):
-            if k < 5:
-                src = grid_ref[4 * k : 4 * k + 4, :, base : base + 128].reshape(128, 128)
-            else:
-                hi, lo = split_hi_lo(dif[:, base : base + 128])
-                src = jnp.concatenate(
-                    [wet[:, base : base + 128], pad, hi, pad, lo, pad, jnp.zeros((32, 128), F32)], axis=0
-                ).astype(BF16)
-            r16, l16 = iota((16, 128), 0), iota((16, 128), 1)
-            pick = onehot(((r16 == k) & (l16 == lane0)) | ((r16 == 8 + k) & (l16 == lane0 + 1)))
-            edge += mm(pick, src, NT)
-        pieces = [edge]
-        for i in range(2):
-            rows = jnp.zeros((8, 128), F32)
-            for e in range(8):
-                rows = jnp.where(row8 == e, wgt_ref[side, e].astype(F32)[14 * side + i : 14 * side + i + 1], rows)
-            pieces.append(rows)
-        blocks.append(jnp.concatenate(pieces, axis=0))
-    for t in range(8):
-        to_left = ((me_lon + 7) & 7) == t
-        block = jnp.where(to_left, blocks[0], blocks[1]).astype(BF16)
-        for g in range(4):
-            out_ref[g * 8 + t, ROW_EDGE:ROW_SENT, :] = block
-            out_ref[g * 8 + t, ROW_SENT:SLOT_ROWS, :] = spread
+            out_ref[g * 8 + t, AREA:SLOT_ROWS, :] = tile[40 * t : 40 * t + 40].astype(BF16)
 
 
 def rim_kernel(wet_hbm, diff_hbm, grid_hbm, up_ref, down_ref, wet_ref, diff_ref, rows_ref, sems):
@@ -170,7 +171,7 @@
 
     lists = [tuple(upright(list_ref[c]) for c in range(3))]
     for slot in (slot_l, slot_r):
-        rows = recv_ref[slot, 32:48, :].astype(F32)[8:16].astype(I32)
+        rows = recv_ref[slot, ROW_LIST : ROW_LIST + 8, :].astype(F32).astype(I32)
         lists.append((rows[:, 0:1], rows[:, 1:2], rows[:, 2:3]))
     pairs = [ids(k, s, me_lon + shift) for (k, s, _), shift in zip(lists, (0, 7, 1))]
     slot_id = jnp.concatenate([p[0] for p in pairs], axis=0)
@@ -179,7 +180,7 @@
     source = jnp.zeros((24, 128), F32)
     for slot in range(32):
         pick = jnp.where(slot_id == slot, in_block, 0.0).astype(BF16)
-        source += mm(pick, recv_ref[slot, ROW_SENT:SLOT_ROWS, :])
+        source += mm(pick, recv_ref[slot, 0:AREA, :])
     own = source[0:8].astype(BF16)
     prod = jnp.zeros((8, 128), F32)
     for e in range(8):
@@ -193,7 +194,7 @@
     lane = iota((8, 128), 1)
     values, spots = [], []
     for n, (slot, lane0, col) in enumerate(((slot_l, 126, 4), (slot_r, 0, 0))):
-        rows = recv_ref[slot, ROW_WGT:ROW_SENT, :].astype(F32)
+        rows = recv_ref[slot, ROW_WGT:ROW_LIST, :].astype(F32)
         src = source[8 + 8 * n : 16 + 8 * n]
         v0 = jnp.sum(rows[0:8] * src, axis=1, keepdims=True)
         v1 = jnp.sum(rows[8:16] * src, axis=1, keepdims=True)
@@ -203,7 +204,7 @@
         spots.append(jnp.where((lane == grow) & (goal - 5 * grow == col), 1.0, 0.0))
     rec_tail = mm(jnp.concatenate(spots, axis=0), jnp.concatenate(values, axis=0), TN, lax.Precision.HIGHEST)[0:20]
     edge = jnp.concatenate(
-        [recv_ref[slot_l, ROW_EDGE:ROW_WGT, :].astype(F32), recv_ref[slot_r, ROW_EDGE:ROW_WGT, :].astype(F32)], axis=0
+        [recv_ref[slot_l, 0:ROW_WGT, :].astype(F32), recv_ref[slot_r, 0:ROW_WGT, :].astype(F32)], axis=0
     ).astype(BF16)
     r32, l32 = iota((32, 128), 0), iota((32, 128), 1)
 
@@ -311,10 +312,10 @@
     norm = np.float32(1.0 / math.sqrt(5120.0))
     sums = []
     for g in range(3):
-        acc = recv_ref[g * 8, 0:48, :].astype(F32)
+        acc = recv_ref[g * 8, AREA:SLOT_ROWS, :].astype(F32)
         for t in range(1, 8):
-            acc += recv_ref[g * 8 + t, 0:48, :].astype(F32)
-        sums.append(acc[0:40])
+            acc += recv_ref[g * 8 + t, AREA:SLOT_ROWS, :].astype(F32)
+        sums.append(acc)
     stack = (jnp.concatenate(sums + [jnp.zeros((8, 128), F32)], axis=0) * norm).astype(BF16)
     out = jnp.zeros((256, 128), F32)
     for j2 in range(2):
@@ -329,16 +330,13 @@
     out_ref[...] = out.astype(BF16)
 
 
-def legendre_kernel(waves_hbm, table_hbm, after_hbm, out_ref, waves_ref, table_ref, sems):
+def legendre_kernel(waves_ref, table_hbm, out_ref, table_ref, sems):
     copies = [
         pltpu.make_async_copy(table_hbm.at[pl.ds(128 * i, 128), :], table_ref.at[pl.ds(128 * i, 128), :], sems.at[i])
         for i in range(15)
     ]
-    first = pltpu.make_async_copy(waves_hbm, waves_ref, sems.at[15])
-    first.start()
     for c in copies:
         c.start()
-    first.wait()
     lane = iota((8, 128), 1)
     waves = [waves_ref[l].astype(F32) for l in range(32)]
     tiles = []
@@ -354,9 +352,12 @@
                 tile = jnp.where((lane >= start) & (lane < start + 20), moved, tile)
         tiles.append(tile)
     out = jnp.zeros((8, 1280), F32)
-    for i in range(15):
-        copies[i].wait()
-        out += mm(tiles[i].astype(BF16), table_ref[128 * i : 128 * i + 128, :])
+    left = jnp.concatenate(tiles, axis=1).astype(BF16)
+    for i in range(0, 15, 2):
+        for c in copies[i : i + 2]:
+            c.wait()
+        k = min(256, 1920 - 128 * i)
+        out += mm(left[:, 128 * i : 128 * i + k], table_ref[128 * i : 128 * i + k, :])
     for j in range(4):
         out_ref[j] = out[2 * j : 2 * j + 2]
 
@@ -427,9 +428,10 @@
         + [pltpu.VMEM((20, 32, 640), F32), pltpu.SemaphoreType.DMA((20,))],
         out_space=HBM, limit=32,
     )
+    table, stepped = lax.optimization_barrier((legendre[0], stepped))
     spectral = call(
-        legendre_kernel, "legendre", (), (), (waves, legendre[0], stepped), [((4, 2, 1280), F32)],
-        scratch=[pltpu.VMEM((32, 8, 128), BF16), pltpu.VMEM((1920, 1280), BF16), pltpu.SemaphoreType.DMA((16,))],
+        legendre_kernel, "legendre", (), (waves,), (table,), [((4, 2, 1280), F32)],
+        scratch=[pltpu.VMEM((1920, 1280), BF16), pltpu.SemaphoreType.DMA((15,))], limit=60,
     )
     return spectral.reshape(1, 4, 2, 1280), received, stepped.transpose(1, 0, 2)
 

time: 94.4 us -> 91.5 us (0.969)
  waiting for transfers between devices: 18.4 us -> 14.9 us
    all_to_all x1, waiting for transfers between devices: 7.34 us -> 3.8 us  [shards(): plane = lax.all_to_all(packed, ('grp', 'lon'), 0, 0, tiled=True)]
  transfers between devices with their start and end apart: 6 -> 6, of which waited for: 5 -> 5; matrix products, arithmetic and copies ran while one was open for 0% -> 0% of each run, Pallas kernels for 11% -> 12%
where the time goes in v3:
time: 91.5 us; the launch traced here: 91 us
  starting transfers between devices  55.2 us (60%)
  Pallas kernels  19.5 us (21%)
  waiting for transfers between devices  14.9 us (16%)
    pallas_call x6, Pallas kernels, call(): pl.pallas_call(kernel, name=name, out_shape=flat if len(flat) > 1 else fl...  19.5 us
    all_to_all x1, starting transfers between devices, shards(): waves = lax.all_to_all(turned.reshape(32, 8, 128), 'lat', 0, 0, tiled=True)  19.2 us
    all_to_all x1, starting transfers between devices, shards(): plane = lax.all_to_all(packed, ('grp', 'lon'), 0, 0, tiled=True)  17.8 us
    ppermute x1, starting transfers between devices, shards(): below = lax.ppermute(up, ('grp', 'lat'), to_before)  9.34 us
    all_to_all x1, waiting for transfers between devices, shards(): waves = lax.all_to_all(turned.reshape(32, 8, 128), 'lat', 0, 0, tiled=True)  7.69 us
    all_to_all x1, waiting for transfers between devices, shards(): plane = lax.all_to_all(packed, ('grp', 'lon'), 0, 0, tiled=True)  3.8 us
    ppermute x1, starting transfers between devices, shards(): below2 = lax.ppermute(up2, ('grp', 'lat'), to_before)  3.63 us
    ppermute x1, starting transfers between devices, shards(): above2 = lax.ppermute(down2, ('grp', 'lat'), to_after)  3.13 us
  transfers between devices with their start and end apart: 6, of which 5 were waited for; matrix products, arithmetic and copies ran while one was open for 0% of the time, Pallas kernels for 12%

profile of v3, /device:TPU:1, one launch (start us, length us, event | category | flops | bytes accessed | tf_op | source)
XLA Modules:
  0.0 91.0 jit_solution(5139073068111383504)
XLA Ops:
  0.6 3.7 %pack.1 = bf16[32,144,128]{2,1,0:T(8,128)(2,1)} custom-call(f32[128,640]{1,0:T(8,128)} %constant.4.clone.cos_hbm, f32[128,640]{1,0:T(8,128)} %constant.5.clone.sin_hbm, s32[3,1,8]{2,1,0:T(1,128)} %bitcast.14, bf16[20,32,640]{2,1,0:T(8,128)(2,1)} %bitcast.9, f32[20,640]{1,0:T(8,128)} %sent_hbm.1, s32[20,640]{1,0:T(8,128)} %wet_ref.1, f32[20,640]{1,0:T(8,128)} %diff_ref.1, ...), custom_call_target="tpu_custom_call" | custom-call | tf_op jit(solution)/shard_map/pack/pallas_call | solution.py:372
  4.4 17.8 %all-to-all-start = ((bf16[32,144,128]{2,1,0:T(8,128)(2,1)}), bf16[32,144,128]{2,1,0:T(8,128)(2,1)S(1)}, u32[]{:S(2)}, u32[]{:S(2)}) async-start(bf16[32,144,128]{2,1,0:T(8,128)(2,1)} %pack.1), calls=%async_computation | async-start | bytes 2359296 | tf_op jit(solution)/shard_map/all_to_all | solution.py:405
  22.1 0.0 copy-start.1
  22.1 0.0 copy-start.2
  22.2 0.0 copy-start.3
  22.2 0.0 copy-start.4
  22.2 1.8 %rim.1 = (bf16[2,40,640]{2,1,0:T(8,128)(2,1)}, bf16[2,40,640]{2,1,0:T(8,128)(2,1)}) custom-call(s32[20,640]{1,0:T(8,128)} %wet_ref.1, f32[20,640]{1,0:T(8,128)} %diff_ref.1, bf16[20,32,640]{2,1,0:T(8,128)(2,1)} %bitcast.10), custom_call_target="tpu_custom_call" | custom-call | tf_op jit(solution)/shard_map/rim/pallas_call | solution.py:372
  24.0 0.0 copy-start
  24.0 2.1 %collective-permute-start = (bf16[2,40,640]{2,1,0:T(8,128)(2,1)}, bf16[2,40,640]{2,1,0:T(8,128)(2,1)S(1)}, u32[]{:S(2)}, u32[]{:S(2)}) collective-permute-start(bf16[2,40,640]{2,1,0:T(8,128)(2,1)} %get-tuple-element.15), channel_id=1, source_target_pairs={{0,8},{8,16},{16,24},{24,32},{32,40},{40,48},{48,56},{56,64},{64,7... | collective-permute-start | bytes 307208 | tf_op jit(solution)/shard_map/ppermute | solution.py:413
  26.0 9.3 %collective-permute-start.1 = (bf16[2,40,640]{2,1,0:T(8,128)(2,1)}, bf16[2,40,640]{2,1,0:T(8,128)(2,1)S(1)}, u32[]{:S(2)}, u32[]{:S(2)}) collective-permute-start(bf16[2,40,640]{2,1,0:T(8,128)(2,1)} %get-tuple-element.16), channel_id=1, source_target_pairs={{8,0},{16,8},{24,16},{32,24},{40,32},{48,40},{56,48},{64,56},{72,6... | collective-permute-start | bytes 307208 | tf_op jit(solution)/shard_map/ppermute | solution.py:412
  35.4 1.6 %collective-permute-done.above_ref = bf16[2,40,640]{2,1,0:T(8,128)(2,1)S(1)} collective-permute-done((bf16[2,40,640]{2,1,0:T(8,128)(2,1)}, bf16[2,40,640]{2,1,0:T(8,128)(2,1)S(1)}, u32[]{:S(2)}, u32[]{:S(2)}) %collective-permute-start) | collective-permute-done | bytes 102432 | tf_op jit(solution)/shard_map/ppermute | solution.py:413
  37.0 0.4 collective-permute-done.1.below_ref
  37.4 3.8 %all-to-all-done.recv_ref = bf16[32,144,128]{2,1,0:T(8,128)(2,1)S(1)} async-done(((bf16[32,144,128]{2,1,0:T(8,128)(2,1)}), bf16[32,144,128]{2,1,0:T(8,128)(2,1)S(1)}, u32[]{:S(2)}, u32[]{:S(2)}) %all-to-all-start) | async-done | bytes 1179680 | tf_op jit(solution)/shard_map/all_to_all | solution.py:405
  41.2 1.0 %turn.1 = bf16[256,128]{1,0:T(8,128)(2,1)} custom-call(bf16[32,144,128]{2,1,0:T(8,128)(2,1)S(1)} %all-to-all-done.recv_ref), custom_call_target="tpu_custom_call" | custom-call | tf_op jit(solution)/shard_map/turn/pallas_call | solution.py:372
  42.1 19.2 %all-to-all-start.1 = ((bf16[32,8,128]{2,1,0:T(8,128)(2,1)}), bf16[32,8,128]{2,1,0:T(8,128)(2,1)S(1)}, u32[]{:S(2)}, u32[]{:S(2)}) async-start(bf16[32,8,128]{2,1,0:T(8,128)(2,1)} %bitcast.4), calls=%async_computation.1 | async-start | bytes 131072 | tf_op jit(solution)/shard_map/all_to_all | solution.py:416
  61.4 0.0 copy-done.1
  61.4 0.0 copy-done.2
  61.4 0.0 copy-done.3
  61.4 0.0 copy-done.4
  61.4 2.1 %remap.1 = (f32[20,640]{1,0:T(8,128)}, bf16[20,32,128]{2,1,0:T(8,128)(2,1)S(1)}, f32[3,20,768]{2,1,0:T(8,128)S(1)}, bf16[2,48,128]{2,1,0:T(8,128)(2,1)S(1)}, bf16[2,48,128]{2,1,0:T(8,128)(2,1)S(1)}) custom-call(s32[3,1,8]{2,1,0:T(1,128)S(1)} %bitcast.15, bf16[32,144,128]{2,1,0:T(8,128)(2,1)S(1)} %all-to-all-done.recv_ref, bf16[8,128,128]{2,1,0:T(8,128)(2,1)S(1)} %bitcast.13, ...), custom_call_target="tpu_custom_call" | custom-call | tf_op jit(solution)/shard_map/remap/pallas_call | solution.py:372
  63.5 3.1 %collective-permute-start.2 = (bf16[2,48,128]{2,1,0:T(8,128)(2,1)S(1)}, bf16[2,48,128]{2,1,0:T(8,128)(2,1)S(1)}, u32[]{:S(2)}, u32[]{:S(2)}) collective-permute-start(bf16[2,48,128]{2,1,0:T(8,128)(2,1)S(1)} %get-tuple-element.22), channel_id=1, source_target_pairs={{0,8},{8,16},{16,24},{24,32},{32,40},{40,48},{48,56},{56,64},{64,7... | collective-permute-start | bytes 73736 | tf_op jit(solution)/shard_map/ppermute | solution.py:423
  66.6 3.6 %collective-permute-start.3 = (bf16[2,48,128]{2,1,0:T(8,128)(2,1)S(1)}, bf16[2,48,128]{2,1,0:T(8,128)(2,1)S(1)}, u32[]{:S(2)}, u32[]{:S(2)}) collective-permute-start(bf16[2,48,128]{2,1,0:T(8,128)(2,1)S(1)} %get-tuple-element.23), channel_id=1, source_target_pairs={{8,0},{16,8},{24,16},{32,24},{40,32},{48,40},{56,48},{64,56},{72,6... | collective-permute-start | bytes 73736 | tf_op jit(solution)/shard_map/ppermute | solution.py:422
  70.3 0.0 collective-permute-done.2.above2_ref
  70.3 1.4 %collective-permute-done.3.below2_ref = bf16[2,48,128]{2,1,0:T(8,128)(2,1)S(1)} collective-permute-done((bf16[2,48,128]{2,1,0:T(8,128)(2,1)S(1)}, bf16[2,48,128]{2,1,0:T(8,128)(2,1)S(1)}, u32[]{:S(2)}, u32[]{:S(2)}) %collective-permute-start.3) | collective-permute-done | bytes 24608 | tf_op jit(solution)/shard_map/ppermute | solution.py:422
  71.7 0.0 copy-done
  71.7 6.8 %step.1 = f32[20,32,640]{2,1,0:T(8,128)} custom-call(bf16[20,32,128]{2,1,0:T(8,128)(2,1)S(1)} %get-tuple-element.18.tail_ref, f32[3,20,768]{2,1,0:T(8,128)S(1)} %get-tuple-element.19.planes_ref, bf16[2,40,640]{2,1,0:T(8,128)(2,1)S(1)} %collective-permute-done.above_ref, bf16[2,40,640]{2,1,0:T(8,128)(2,1)S(1)} %collective-permute-done.1.below_ref, ...), custom_call_target="tpu_custom_call" | custom-call | tf_op jit(solution)/shard_map/step/pallas_call | solution.py:372
  78.5 7.7 %all-to-all-done.1.waves_ref = bf16[32,8,128]{2,1,0:T(8,128)(2,1)S(1)} async-done(((bf16[32,8,128]{2,1,0:T(8,128)(2,1)}), bf16[32,8,128]{2,1,0:T(8,128)(2,1)S(1)}, u32[]{:S(2)}, u32[]{:S(2)}) %all-to-all-start.1) | async-done | bytes 65568 | tf_op jit(solution)/shard_map/all_to_all | solution.py:416
  86.2 0.0 copy-start.5
  86.2 0.6 copy-done.5
  86.8 4.2 %legendre.1 = f32[4,2,1280]{2,1,0:T(2,128)} custom-call(bf16[32,8,128]{2,1,0:T(8,128)(2,1)} %copy-done.5, bf16[1920,1280]{1,0:T(8,128)(2,1)} %bitcast.16), custom_call_target="tpu_custom_call" | custom-call | tf_op jit(solution)/shard_map/legendre/pallas_call | solution.py:372
Async XLA Ops:
  4.4 36.8 %all-to-all-start = ((bf16[32,144,128]{2,1,0:T(8,128)(2,1)}), bf16[32,144,128]{2,1,0:T(8,128)(2,1)S(1)}, u32[]{:S(2)}, u32[]{:S(2)}) async-start(bf16[32,144,128]{2,1,0:T(8,128)(2,1)} %pack.1), calls=%async_computation | async-start | bytes 2359296 | tf_op jit(solution)/shard_map/all_to_all | solution.py:405
  22.1 39.2 %copy-start.1 = (bf16[1,1,8,128,128]{4,3,2,1,0:T(8,128)(2,1)S(1)}, bf16[1,1,8,128,128]{4,3,2,1,0:T(8,128)(2,1)}, u32[]{:S(2)}) copy-start(bf16[1,1,8,128,128]{4,3,2,1,0:T(8,128)(2,1)} %param.15) | copy-start | bytes 786436
  22.1 39.2 %copy-start.2 = (s32[20,640]{1,0:T(8,128)S(1)}, s32[20,640]{1,0:T(8,128)}, u32[]{:S(2)}) copy-start(s32[20,640]{1,0:T(8,128)} %wet_ref.1) | copy-start | bytes 153604
  22.2 39.2 %copy-start.3 = (f32[20,640]{1,0:T(8,128)S(1)}, f32[20,640]{1,0:T(8,128)}, u32[]{:S(2)}) copy-start(f32[20,640]{1,0:T(8,128)} %diff_ref.1) | copy-start | bytes 153604
  22.2 39.2 %copy-start.4 = (s32[1,1,8,3]{2,1,3,0:T(1,128)S(1)}, s32[1,1,8,3]{2,1,3,0:T(1,128)}, u32[]{:S(2)}) copy-start(s32[1,1,8,3]{2,1,3,0:T(1,128)} %param.14) | copy-start | bytes 292
  24.0 47.8 %copy-start = (bf16[32,20,640]{2,0,1:T(8,128)(2,1)S(1)}, bf16[32,20,640]{2,0,1:T(8,128)(2,1)}, u32[]{:S(2)}) copy-start(bf16[32,20,640]{2,0,1:T(8,128)(2,1)} %param.9) | copy-start | bytes 2457604
  24.0 13.0 %collective-permute-start = (bf16[2,40,640]{2,1,0:T(8,128)(2,1)}, bf16[2,40,640]{2,1,0:T(8,128)(2,1)S(1)}, u32[]{:S(2)}, u32[]{:S(2)}) collective-permute-start(bf16[2,40,640]{2,1,0:T(8,128)(2,1)} %get-tuple-element.15), channel_id=1, source_target_pairs={{0,8},{8,16},{16,24},{24,32},{32,40},{40,48},{48,56},{56,64},{64,7... | collective-permute-start | bytes 307208 | tf_op jit(solution)/shard_map/ppermute | solution.py:413
  26.0 11.3 %collective-permute-start.1 = (bf16[2,40,640]{2,1,0:T(8,128)(2,1)}, bf16[2,40,640]{2,1,0:T(8,128)(2,1)S(1)}, u32[]{:S(2)}, u32[]{:S(2)}) collective-permute-start(bf16[2,40,640]{2,1,0:T(8,128)(2,1)} %get-tuple-element.16), channel_id=1, source_target_pairs={{8,0},{16,8},{24,16},{32,24},{40,32},{48,40},{56,48},{64,56},{72,6... | collective-permute-start | bytes 307208 | tf_op jit(solution)/shard_map/ppermute | solution.py:412
  42.1 44.0 %all-to-all-start.1 = ((bf16[32,8,128]{2,1,0:T(8,128)(2,1)}), bf16[32,8,128]{2,1,0:T(8,128)(2,1)S(1)}, u32[]{:S(2)}, u32[]{:S(2)}) async-start(bf16[32,8,128]{2,1,0:T(8,128)(2,1)} %bitcast.4), calls=%async_computation.1 | async-start | bytes 131072 | tf_op jit(solution)/shard_map/all_to_all | solution.py:416
  63.5 6.8 %collective-permute-start.2 = (bf16[2,48,128]{2,1,0:T(8,128)(2,1)S(1)}, bf16[2,48,128]{2,1,0:T(8,128)(2,1)S(1)}, u32[]{:S(2)}, u32[]{:S(2)}) collective-permute-start(bf16[2,48,128]{2,1,0:T(8,128)(2,1)S(1)} %get-tuple-element.22), channel_id=1, source_target_pairs={{0,8},{8,16},{16,24},{24,32},{32,40},{40,48},{48,56},{56,64},{64,7... | collective-permute-start | bytes 73736 | tf_op jit(solution)/shard_map/ppermute | solution.py:423
  66.6 5.1 %collective-permute-start.3 = (bf16[2,48,128]{2,1,0:T(8,128)(2,1)S(1)}, bf16[2,48,128]{2,1,0:T(8,128)(2,1)S(1)}, u32[]{:S(2)}, u32[]{:S(2)}) collective-permute-start(bf16[2,48,128]{2,1,0:T(8,128)(2,1)S(1)} %get-tuple-element.23), channel_id=1, source_target_pairs={{8,0},{16,8},{24,16},{32,24},{40,32},{48,40},{56,48},{64,56},{72,6... | collective-permute-start | bytes 73736 | tf_op jit(solution)/shard_map/ppermute | solution.py:422
  86.2 0.6 copy-start.5

commit v4 on v3

--- a/solution.py
+++ b/solution.py
@@ -19,6 +19,7 @@
 ROW_WGT = 16
 ROW_LIST = 32
 AREA = 104
+FIRST_LAT = 16
 SLOT_ROWS = 144
 
 
@@ -324,21 +325,24 @@
         pick = onehot((iota((128, 128), 1) == lane + 20 * g + 20 * j2) & (lane < 60))
         lined = mm(pick, stack).astype(BF16)
         rho, lam = iota((256, 128), 0), iota((256, 128), 1)
-        want = ((rho >> 2) & 1) * 64 + (rho & 1) * 32 + (rho >> 3)
+        want = ((rho >> 2) & 1) * 64 + (rho & 1) * 32 + (((rho >> 3) + FIRST_LAT) & 31)
         place = onehot((((rho >> 1) & 1) == j2) & (lam == want))
         out += mm(place, lined, NT)
     out_ref[...] = out.astype(BF16)
 
 
-def legendre_kernel(waves_ref, table_hbm, out_ref, table_ref, sems):
+def legendre_kernel(waves_hbm, table_hbm, out_ref, waves_ref, table_ref, sems):
     copies = [
         pltpu.make_async_copy(table_hbm.at[pl.ds(128 * i, 128), :], table_ref.at[pl.ds(128 * i, 128), :], sems.at[i])
         for i in range(15)
     ]
+    first = pltpu.make_async_copy(waves_hbm, waves_ref, sems.at[15])
+    first.start()
     for c in copies:
         c.start()
+    first.wait()
     lane = iota((8, 128), 1)
-    waves = [waves_ref[l].astype(F32) for l in range(32)]
+    waves = [waves_ref[(l - FIRST_LAT) % 32].astype(F32) for l in range(32)]
     tiles = []
     for tau in range(15):
         tile = jnp.zeros((8, 128), F32)
@@ -352,12 +356,9 @@
                 tile = jnp.where((lane >= start) & (lane < start + 20), moved, tile)
         tiles.append(tile)
     out = jnp.zeros((8, 1280), F32)
-    left = jnp.concatenate(tiles, axis=1).astype(BF16)
-    for i in range(0, 15, 2):
-        for c in copies[i : i + 2]:
-            c.wait()
-        k = min(256, 1920 - 128 * i)
-        out += mm(left[:, 128 * i : 128 * i + k], table_ref[128 * i : 128 * i + k, :])
+    for i in range(15):
+        copies[i].wait()
+        out += mm(tiles[i].astype(BF16), table_ref[128 * i : 128 * i + 128, :])
     for j in range(4):
         out_ref[j] = out[2 * j : 2 * j + 2]
 
@@ -413,7 +414,9 @@
     above = lax.ppermute(down, ("grp", "lat"), to_after)
     plane, above, below = lax.optimization_barrier((plane, above, below))
     turned = call(turn_kernel, "turn", (), (plane,), (), [((256, 128), BF16)], limit=16)
-    waves = lax.all_to_all(turned.reshape(32, 8, 128), "lat", 0, 0, tiled=True)
+    waves = lax.all_to_all(
+        turned.reshape(32, 8, 128), "lat", 0, 0, tiled=True, axis_index_groups=[[(i + FIRST_LAT) % 32 for i in range(32)]]
+    )
     received, tail, planes, up2, down2 = call(
         remap_kernel, "remap", (), (listing, plane, weights, wet_mask, diffusivity), (),
         [((20, 640), F32), ((20, 32, 128), BF16), ((3, 20, WIDE), F32), ((2, 48, 128), BF16), ((2, 48, 128), BF16)],
@@ -430,8 +433,8 @@
     )
     table, stepped = lax.optimization_barrier((legendre[0], stepped))
     spectral = call(
-        legendre_kernel, "legendre", (), (waves,), (table,), [((4, 2, 1280), F32)],
-        scratch=[pltpu.VMEM((1920, 1280), BF16), pltpu.SemaphoreType.DMA((15,))], limit=60,
+        legendre_kernel, "legendre", (), (), (waves, table), [((4, 2, 1280), F32)],
+        scratch=[pltpu.VMEM((32, 8, 128), BF16), pltpu.VMEM((1920, 1280), BF16), pltpu.SemaphoreType.DMA((16,))],
     )
     return spectral.reshape(1, 4, 2, 1280), received, stepped.transpose(1, 0, 2)
 

time: 91.5 us -> 89.5 us (0.978)
  waiting for transfers between devices: 14.9 us -> 6.69 us
  starting transfers between devices: 55.2 us -> 62 us
    all_to_all x1, waiting for transfers between devices: 7.69 us -> 0.01 us  [shards(): lax.all_to_all(turned.reshape(32, 8, 128), 'lat', 0, 0, tiled=True, axis_...]
    all_to_all x1, starting transfers between devices: 19.2 us -> 26.1 us  [shards(): lax.all_to_all(turned.reshape(32, 8, 128), 'lat', 0, 0, tiled=True, axis_...]
    ppermute x1, starting transfers between devices: 3.13 us -> 2.18 us  [shards(): above2 = lax.ppermute(down2, ('grp', 'lat'), to_after)]
    ppermute x1, starting transfers between devices: 3.63 us -> 4.58 us  [shards(): below2 = lax.ppermute(up2, ('grp', 'lat'), to_before)]
  transfers between devices with their start and end apart: 6 -> 6, of which waited for: 5 -> 4; matrix products, arithmetic and copies ran while one was open for 0% -> 0% of each run, Pallas kernels for 12% -> 12%
where the time goes in v4:
time: 89.5 us; the launch traced here: 88.8 us
  starting transfers between devices  62 us (69%)
  Pallas kernels  18.6 us (21%)
  waiting for transfers between devices  6.69 us (7%)
    all_to_all x1, starting transfers between devices, shards(): lax.all_to_all(turned.reshape(32, 8, 128), 'lat', 0, 0, tiled=True, axis_...  26.1 us
    pallas_call x6, Pallas kernels, call(): pl.pallas_call(kernel, name=name, out_shape=flat if len(flat) > 1 else fl...  18.6 us
    all_to_all x1, starting transfers between devices, shards(): plane = lax.all_to_all(packed, ('grp', 'lon'), 0, 0, tiled=True)  17.8 us
    ppermute x1, starting transfers between devices, shards(): below = lax.ppermute(up, ('grp', 'lat'), to_before)  9.34 us
    ppermute x1, starting transfers between devices, shards(): below2 = lax.ppermute(up2, ('grp', 'lat'), to_before)  4.58 us
    all_to_all x1, waiting for transfers between devices, shards(): plane = lax.all_to_all(packed, ('grp', 'lon'), 0, 0, tiled=True)  3.8 us
    ppermute x1, starting transfers between devices, shards(): above2 = lax.ppermute(down2, ('grp', 'lat'), to_after)  2.18 us
    ppermute x1, starting transfers between devices, shards(): above = lax.ppermute(down, ('grp', 'lat'), to_after)  2.05 us
  transfers between devices with their start and end apart: 6, of which 4 were waited for; matrix products, arithmetic and copies ran while one was open for 0% of the time, Pallas kernels for 12%

profile of v4, /device:TPU:1, one launch (start us, length us, event | category | flops | bytes accessed | tf_op | source)
XLA Modules:
  0.0 88.8 jit_solution(2035066156536590822)
XLA Ops:
  0.6 3.7 %pack.1 = bf16[32,144,128]{2,1,0:T(8,128)(2,1)} custom-call(f32[128,640]{1,0:T(8,128)} %constant.4.clone.cos_hbm, f32[128,640]{1,0:T(8,128)} %constant.5.clone.sin_hbm, s32[3,1,8]{2,1,0:T(1,128)} %bitcast.14, bf16[20,32,640]{2,1,0:T(8,128)(2,1)} %bitcast.9, f32[20,640]{1,0:T(8,128)} %sent_hbm.1, s32[20,640]{1,0:T(8,128)} %wet_ref.1, f32[20,640]{1,0:T(8,128)} %diff_ref.1, ...), custom_call_target="tpu_custom_call" | custom-call | tf_op jit(solution)/shard_map/pack/pallas_call | solution.py:373
  4.4 17.8 %all-to-all-start = ((bf16[32,144,128]{2,1,0:T(8,128)(2,1)}), bf16[32,144,128]{2,1,0:T(8,128)(2,1)S(1)}, u32[]{:S(2)}, u32[]{:S(2)}) async-start(bf16[32,144,128]{2,1,0:T(8,128)(2,1)} %pack.1), calls=%async_computation | async-start | bytes 2359296 | tf_op jit(solution)/shard_map/all_to_all | solution.py:406
  22.1 0.0 copy-start.1
  22.1 0.0 copy-start.2
  22.2 0.0 copy-start.3
  22.2 0.0 copy-start.4
  22.2 1.8 %rim.1 = (bf16[2,40,640]{2,1,0:T(8,128)(2,1)}, bf16[2,40,640]{2,1,0:T(8,128)(2,1)}) custom-call(s32[20,640]{1,0:T(8,128)} %wet_ref.1, f32[20,640]{1,0:T(8,128)} %diff_ref.1, bf16[20,32,640]{2,1,0:T(8,128)(2,1)} %bitcast.10), custom_call_target="tpu_custom_call" | custom-call | tf_op jit(solution)/shard_map/rim/pallas_call | solution.py:373
  24.0 0.0 copy-start
  24.0 2.1 %collective-permute-start = (bf16[2,40,640]{2,1,0:T(8,128)(2,1)}, bf16[2,40,640]{2,1,0:T(8,128)(2,1)S(1)}, u32[]{:S(2)}, u32[]{:S(2)}) collective-permute-start(bf16[2,40,640]{2,1,0:T(8,128)(2,1)} %get-tuple-element.15), channel_id=1, source_target_pairs={{0,8},{8,16},{16,24},{24,32},{32,40},{40,48},{48,56},{56,64},{64,7... | collective-permute-start | bytes 307208 | tf_op jit(solution)/shard_map/ppermute | solution.py:414
  26.0 9.3 %collective-permute-start.1 = (bf16[2,40,640]{2,1,0:T(8,128)(2,1)}, bf16[2,40,640]{2,1,0:T(8,128)(2,1)S(1)}, u32[]{:S(2)}, u32[]{:S(2)}) collective-permute-start(bf16[2,40,640]{2,1,0:T(8,128)(2,1)} %get-tuple-element.16), channel_id=1, source_target_pairs={{8,0},{16,8},{24,16},{32,24},{40,32},{48,40},{56,48},{64,56},{72,6... | collective-permute-start | bytes 307208 | tf_op jit(solution)/shard_map/ppermute | solution.py:413
  35.4 1.6 %collective-permute-done.above_ref = bf16[2,40,640]{2,1,0:T(8,128)(2,1)S(1)} collective-permute-done((bf16[2,40,640]{2,1,0:T(8,128)(2,1)}, bf16[2,40,640]{2,1,0:T(8,128)(2,1)S(1)}, u32[]{:S(2)}, u32[]{:S(2)}) %collective-permute-start) | collective-permute-done | bytes 102432 | tf_op jit(solution)/shard_map/ppermute | solution.py:414
  37.0 0.4 collective-permute-done.1.below_ref
  37.4 3.8 %all-to-all-done.recv_ref = bf16[32,144,128]{2,1,0:T(8,128)(2,1)S(1)} async-done(((bf16[32,144,128]{2,1,0:T(8,128)(2,1)}), bf16[32,144,128]{2,1,0:T(8,128)(2,1)S(1)}, u32[]{:S(2)}, u32[]{:S(2)}) %all-to-all-start) | async-done | bytes 1179680 | tf_op jit(solution)/shard_map/all_to_all | solution.py:406
  41.2 1.0 %turn.1 = bf16[256,128]{1,0:T(8,128)(2,1)} custom-call(bf16[32,144,128]{2,1,0:T(8,128)(2,1)S(1)} %all-to-all-done.recv_ref), custom_call_target="tpu_custom_call" | custom-call | tf_op jit(solution)/shard_map/turn/pallas_call | solution.py:373
  42.2 26.1 %all-to-all-start.1 = ((bf16[32,8,128]{2,1,0:T(8,128)(2,1)}), bf16[32,8,128]{2,1,0:T(8,128)(2,1)S(1)}, u32[]{:S(2)}, u32[]{:S(2)}) async-start(bf16[32,8,128]{2,1,0:T(8,128)(2,1)} %bitcast.4), calls=%async_computation.1 | async-start | bytes 131072 | tf_op jit(solution)/shard_map/all_to_all | solution.py:417
  68.3 0.0 copy-done.1
  68.3 0.0 copy-done.2
  68.3 0.0 copy-done.3
  68.3 0.0 copy-done.4
  68.3 2.1 %remap.1 = (f32[20,640]{1,0:T(8,128)}, bf16[20,32,128]{2,1,0:T(8,128)(2,1)S(1)}, f32[3,20,768]{2,1,0:T(8,128)S(1)}, bf16[2,48,128]{2,1,0:T(8,128)(2,1)S(1)}, bf16[2,48,128]{2,1,0:T(8,128)(2,1)S(1)}) custom-call(s32[3,1,8]{2,1,0:T(1,128)S(1)} %bitcast.15, bf16[32,144,128]{2,1,0:T(8,128)(2,1)S(1)} %all-to-all-done.recv_ref, bf16[8,128,128]{2,1,0:T(8,128)(2,1)S(1)} %bitcast.13, ...), custom_call_target="tpu_custom_call" | custom-call | tf_op jit(solution)/shard_map/remap/pallas_call | solution.py:373
  70.4 2.2 %collective-permute-start.2 = (bf16[2,48,128]{2,1,0:T(8,128)(2,1)S(1)}, bf16[2,48,128]{2,1,0:T(8,128)(2,1)S(1)}, u32[]{:S(2)}, u32[]{:S(2)}) collective-permute-start(bf16[2,48,128]{2,1,0:T(8,128)(2,1)S(1)} %get-tuple-element.22), channel_id=1, source_target_pairs={{0,8},{8,16},{16,24},{24,32},{32,40},{40,48},{48,56},{56,64},{64,7... | collective-permute-start | bytes 73736 | tf_op jit(solution)/shard_map/ppermute | solution.py:426
  72.6 4.6 %collective-permute-start.3 = (bf16[2,48,128]{2,1,0:T(8,128)(2,1)S(1)}, bf16[2,48,128]{2,1,0:T(8,128)(2,1)S(1)}, u32[]{:S(2)}, u32[]{:S(2)}) collective-permute-start(bf16[2,48,128]{2,1,0:T(8,128)(2,1)S(1)} %get-tuple-element.23), channel_id=1, source_target_pairs={{8,0},{16,8},{24,16},{32,24},{40,32},{48,40},{56,48},{64,56},{72,6... | collective-permute-start | bytes 73736 | tf_op jit(solution)/shard_map/ppermute | solution.py:425
  77.2 0.0 collective-permute-done.2.above2_ref
  77.2 0.9 %collective-permute-done.3.below2_ref = bf16[2,48,128]{2,1,0:T(8,128)(2,1)S(1)} collective-permute-done((bf16[2,48,128]{2,1,0:T(8,128)(2,1)S(1)}, bf16[2,48,128]{2,1,0:T(8,128)(2,1)S(1)}, u32[]{:S(2)}, u32[]{:S(2)}) %collective-permute-start.3) | collective-permute-done | bytes 24608 | tf_op jit(solution)/shard_map/ppermute | solution.py:425
  78.1 0.0 copy-done
  78.1 6.8 %step.1 = f32[20,32,640]{2,1,0:T(8,128)} custom-call(bf16[20,32,128]{2,1,0:T(8,128)(2,1)S(1)} %get-tuple-element.18.tail_ref, f32[3,20,768]{2,1,0:T(8,128)S(1)} %get-tuple-element.19.planes_ref, bf16[2,40,640]{2,1,0:T(8,128)(2,1)S(1)} %collective-permute-done.above_ref, bf16[2,40,640]{2,1,0:T(8,128)(2,1)S(1)} %collective-permute-done.1.below_ref, ...), custom_call_target="tpu_custom_call" | custom-call | tf_op jit(solution)/shard_map/step/pallas_call | solution.py:373
  84.9 0.0 all-to-all-done.1.waves_hbm
  84.9 0.0 copy-start.5
  84.9 0.6 copy-done.5
  85.5 3.3 %legendre.1 = f32[4,2,1280]{2,1,0:T(2,128)} custom-call(bf16[32,8,128]{2,1,0:T(8,128)(2,1)} %copy-done.5, bf16[1920,1280]{1,0:T(8,128)(2,1)} %bitcast.16), custom_call_target="tpu_custom_call" | custom-call | tf_op jit(solution)/shard_map/legendre/pallas_call | solution.py:373
Async XLA Ops:
  4.4 36.8 %all-to-all-start = ((bf16[32,144,128]{2,1,0:T(8,128)(2,1)}), bf16[32,144,128]{2,1,0:T(8,128)(2,1)S(1)}, u32[]{:S(2)}, u32[]{:S(2)}) async-start(bf16[32,144,128]{2,1,0:T(8,128)(2,1)} %pack.1), calls=%async_computation | async-start | bytes 2359296 | tf_op jit(solution)/shard_map/all_to_all | solution.py:406
  22.1 46.1 %copy-start.1 = (bf16[1,1,8,128,128]{4,3,2,1,0:T(8,128)(2,1)S(1)}, bf16[1,1,8,128,128]{4,3,2,1,0:T(8,128)(2,1)}, u32[]{:S(2)}) copy-start(bf16[1,1,8,128,128]{4,3,2,1,0:T(8,128)(2,1)} %param.15) | copy-start | bytes 786436
  22.1 46.1 %copy-start.2 = (s32[20,640]{1,0:T(8,128)S(1)}, s32[20,640]{1,0:T(8,128)}, u32[]{:S(2)}) copy-start(s32[20,640]{1,0:T(8,128)} %wet_ref.1) | copy-start | bytes 153604
  22.2 46.1 %copy-start.3 = (f32[20,640]{1,0:T(8,128)S(1)}, f32[20,640]{1,0:T(8,128)}, u32[]{:S(2)}) copy-start(f32[20,640]{1,0:T(8,128)} %diff_ref.1) | copy-start | bytes 153604
  22.2 46.1 %copy-start.4 = (s32[1,1,8,3]{2,1,3,0:T(1,128)S(1)}, s32[1,1,8,3]{2,1,3,0:T(1,128)}, u32[]{:S(2)}) copy-start(s32[1,1,8,3]{2,1,3,0:T(1,128)} %param.14) | copy-start | bytes 292
  24.0 54.1 %copy-start = (bf16[32,20,640]{2,0,1:T(8,128)(2,1)S(1)}, bf16[32,20,640]{2,0,1:T(8,128)(2,1)}, u32[]{:S(2)}) copy-start(bf16[32,20,640]{2,0,1:T(8,128)(2,1)} %param.9) | copy-start | bytes 2457604
  24.0 13.0 %collective-permute-start = (bf16[2,40,640]{2,1,0:T(8,128)(2,1)}, bf16[2,40,640]{2,1,0:T(8,128)(2,1)S(1)}, u32[]{:S(2)}, u32[]{:S(2)}) collective-permute-start(bf16[2,40,640]{2,1,0:T(8,128)(2,1)} %get-tuple-element.15), channel_id=1, source_target_pairs={{0,8},{8,16},{16,24},{24,32},{32,40},{40,48},{48,56},{56,64},{64,7... | collective-permute-start | bytes 307208 | tf_op jit(solution)/shard_map/ppermute | solution.py:414
  26.0 11.3 %collective-permute-start.1 = (bf16[2,40,640]{2,1,0:T(8,128)(2,1)}, bf16[2,40,640]{2,1,0:T(8,128)(2,1)S(1)}, u32[]{:S(2)}, u32[]{:S(2)}) collective-permute-start(bf16[2,40,640]{2,1,0:T(8,128)(2,1)} %get-tuple-element.16), channel_id=1, source_target_pairs={{8,0},{16,8},{24,16},{32,24},{40,32},{48,40},{56,48},{64,56},{72,6... | collective-permute-start | bytes 307208 | tf_op jit(solution)/shard_map/ppermute | solution.py:413
  42.2 42.7 %all-to-all-start.1 = ((bf16[32,8,128]{2,1,0:T(8,128)(2,1)}), bf16[32,8,128]{2,1,0:T(8,128)(2,1)S(1)}, u32[]{:S(2)}, u32[]{:S(2)}) async-start(bf16[32,8,128]{2,1,0:T(8,128)(2,1)} %bitcast.4), calls=%async_computation.1 | async-start | bytes 131072 | tf_op jit(solution)/shard_map/all_to_all | solution.py:417
  70.4 6.8 %collective-permute-start.2 = (bf16[2,48,128]{2,1,0:T(8,128)(2,1)S(1)}, bf16[2,48,128]{2,1,0:T(8,128)(2,1)S(1)}, u32[]{:S(2)}, u32[]{:S(2)}) collective-permute-start(bf16[2,48,128]{2,1,0:T(8,128)(2,1)S(1)} %get-tuple-element.22), channel_id=1, source_target_pairs={{0,8},{8,16},{16,24},{24,32},{32,40},{40,48},{48,56},{56,64},{64,7... | collective-permute-start | bytes 73736 | tf_op jit(solution)/shard_map/ppermute | solution.py:426
  72.6 5.5 %collective-permute-start.3 = (bf16[2,48,128]{2,1,0:T(8,128)(2,1)S(1)}, bf16[2,48,128]{2,1,0:T(8,128)(2,1)S(1)}, u32[]{:S(2)}, u32[]{:S(2)}) collective-permute-start(bf16[2,48,128]{2,1,0:T(8,128)(2,1)S(1)} %get-tuple-element.23), channel_id=1, source_target_pairs={{8,0},{16,8},{24,16},{32,24},{40,32},{48,40},{56,48},{64,56},{72,6... | collective-permute-start | bytes 73736 | tf_op jit(solution)/shard_map/ppermute | solution.py:425
  84.9 0.6 copy-start.5

commit v5 on v4

--- a/solution.py
+++ b/solution.py
@@ -19,7 +19,7 @@
 ROW_WGT = 16
 ROW_LIST = 32
 AREA = 104
-FIRST_LAT = 16
+FIRST_LAT = 23
 SLOT_ROWS = 144
 
 
@@ -45,7 +45,7 @@
 
 
 def pack_kernel(cos_hbm, sin_hbm, list_hbm, grid_hbm, sent_hbm, wet_hbm, diff_hbm, wgt_hbm,
-                out_ref, cos_ref, sin_ref, list_ref, grid_ref, sent_ref, wet_ref, diff_ref, wgt_ref, sems):
+                out_hbm, out_ref, cos_ref, sin_ref, list_ref, grid_ref, sent_ref, wet_ref, diff_ref, wgt_ref, sems, out_sems):
     pairs = [(list_hbm, list_ref), (sent_hbm, sent_ref), (wet_hbm, wet_ref), (diff_hbm, diff_ref)]
     pairs += [(wgt_hbm.at[:, pl.ds(112 * side, 16), :], wgt_ref.at[side]) for side in range(2)]
     pairs += [(cos_hbm, cos_ref), (sin_hbm, sin_ref), (grid_hbm, grid_ref)]
@@ -121,6 +121,13 @@
             edge += mm(pick, src, NT)
         pieces = [edge, wgt[2 * side], wgt[2 * side + 1], listing, jnp.zeros((AREA - 40, 128), F32)]
         blocks.append(jnp.concatenate(pieces, axis=0))
+    area = pltpu.make_async_copy(out_ref.at[:, 0:AREA, :], out_hbm.at[:, 0:AREA, :], out_sems.at[4])
+    waves = [
+        pltpu.make_async_copy(
+            out_ref.at[8 * g : 8 * g + 8, AREA:SLOT_ROWS, :], out_hbm.at[8 * g : 8 * g + 8, AREA:SLOT_ROWS, :], out_sems.at[g]
+        )
+        for g in range(4)
+    ]
     for g in range(4):
         same = lax.axis_index("grp") == g
         left = jnp.where(same, blocks[0], spread)
@@ -128,12 +135,16 @@
         for t in range(8):
             to_left = ((me_lon + 7) & 7) == t
             out_ref[g * 8 + t, 0:AREA, :] = jnp.where(to_left, left, right).astype(BF16)
+    area.start()
     moved = mm(order, sums)
     low, high = moved[:320], moved[320:]
     for g in range(4):
         tile = jnp.concatenate([low[:, 64 * g : 64 * g + 64], high[:, 64 * g : 64 * g + 64]], axis=1)
         for t in range(8):
             out_ref[g * 8 + t, AREA:SLOT_ROWS, :] = tile[40 * t : 40 * t + 40].astype(BF16)
+        waves[g].start()
+    for c in waves + [area]:
+        c.wait()
 
 
 def rim_kernel(wet_hbm, diff_hbm, grid_hbm, up_ref, down_ref, wet_ref, diff_ref, rows_ref, sems):
@@ -284,7 +295,7 @@
             u1_ref[r, lev, :] = q * wet
         return carry
 
-    lax.fori_loop(1, 23, first, 0)
+    lax.fori_loop(1, 23, first, 0, unroll=2)
 
     def copy(r):
         return pltpu.make_async_copy(res_ref.at[r], out_hbm.at[r], sems.at[r])
@@ -300,7 +311,7 @@
         copy(r - 2).start()
         return carry
 
-    lax.fori_loop(2, 22, second, 0)
+    lax.fori_loop(2, 22, second, 0, unroll=2)
 
     def finish(r, carry):
         copy(r).wait()
@@ -399,9 +410,10 @@
         pack_kernel, "pack", (), (),
         (jnp.asarray(cos0), jnp.asarray(sin0), listing, rows, sent_field, wet_mask, diffusivity, weights),
         [((32, SLOT_ROWS, 128), BF16)],
-        scratch=[pltpu.VMEM((128, 640), F32), pltpu.VMEM((128, 640), F32), pltpu.VMEM((3, 1, 8), I32), pltpu.VMEM((20, 32, 640), BF16),
+        scratch=[pltpu.VMEM((32, SLOT_ROWS, 128), BF16), pltpu.VMEM((128, 640), F32), pltpu.VMEM((128, 640), F32), pltpu.VMEM((3, 1, 8), I32), pltpu.VMEM((20, 32, 640), BF16),
                  pltpu.VMEM((20, 640), F32), pltpu.VMEM((20, 640), I32), pltpu.VMEM((20, 640), F32),
-                 pltpu.VMEM((2, 8, 16, 128), BF16), pltpu.SemaphoreType.DMA((9,))],
+                 pltpu.VMEM((2, 8, 16, 128), BF16), pltpu.SemaphoreType.DMA((9,)), pltpu.SemaphoreType.DMA((5,))],
+        out_space=HBM,
     )
     plane = lax.all_to_all(packed, ("grp", "lon"), 0, 0, tiled=True)
     up, down = call(

time: 89.5 us -> 82 us (0.916)
  starting transfers between devices: 62 us -> 55.2 us
  Pallas kernels: 18.6 us -> 16.8 us
    all_to_all x1, starting transfers between devices: 26.1 us -> 19.3 us  [shards(): lax.all_to_all(turned.reshape(32, 8, 128), 'lat', 0, 0, tiled=True, axis_...]
    pallas_call x6, Pallas kernels: 18.6 us -> 16.8 us  [call(): pl.pallas_call(kernel, name=name, out_shape=flat if len(flat) > 1 else fl...]
    ppermute x1, starting transfers between devices: 2.18 us -> 3.08 us  [shards(): above2 = lax.ppermute(down2, ('grp', 'lat'), to_after)]
    ppermute x1, starting transfers between devices: 4.58 us -> 3.68 us  [shards(): below2 = lax.ppermute(up2, ('grp', 'lat'), to_before)]
  transfers between devices with their start and end apart: 6 -> 6, of which waited for: 4 -> 4; matrix products, arithmetic and copies ran while one was open for 0% -> 0% of each run, Pallas kernels for 12% -> 11%
where the time goes in v5:
time: 82 us; the launch traced here: 80.7 us
  starting transfers between devices  55.2 us (67%)
  Pallas kernels  16.8 us (20%)
  waiting for transfers between devices  7.21 us (9%)
    all_to_all x1, starting transfers between devices, shards(): lax.all_to_all(turned.reshape(32, 8, 128), 'lat', 0, 0, tiled=True, axis_...  19.3 us
    all_to_all x1, starting transfers between devices, shards(): plane = lax.all_to_all(packed, ('grp', 'lon'), 0, 0, tiled=True)  17.8 us
    pallas_call x6, Pallas kernels, call(): pl.pallas_call(kernel, name=name, out_shape=flat if len(flat) > 1 else fl...  16.8 us
    ppermute x1, starting transfers between devices, shards(): below = lax.ppermute(up, ('grp', 'lat'), to_before)  9.34 us
    all_to_all x1, waiting for transfers between devices, shards(): plane = lax.all_to_all(packed, ('grp', 'lon'), 0, 0, tiled=True)  3.8 us
    ppermute x1, starting transfers between devices, shards(): below2 = lax.ppermute(up2, ('grp', 'lat'), to_before)  3.68 us
    ppermute x1, starting transfers between devices, shards(): above2 = lax.ppermute(down2, ('grp', 'lat'), to_after)  3.08 us
    ppermute x1, starting transfers between devices, shards(): above = lax.ppermute(down, ('grp', 'lat'), to_after)  2.05 us
  transfers between devices with their start and end apart: 6, of which 4 were waited for; matrix products, arithmetic and copies ran while one was open for 0% of the time, Pallas kernels for 11%

profile of v5, /device:TPU:1, one launch (start us, length us, event | category | flops | bytes accessed | tf_op | source)
XLA Modules:
  0.0 80.7 jit_solution(5211130164090480545)
XLA Ops:
  0.6 3.5 %pack.1 = bf16[32,144,128]{2,1,0:T(8,128)(2,1)} custom-call(f32[128,640]{1,0:T(8,128)} %constant.4.clone.cos_hbm, f32[128,640]{1,0:T(8,128)} %constant.5.clone.sin_hbm, s32[3,1,8]{2,1,0:T(1,128)} %bitcast.14, bf16[20,32,640]{2,1,0:T(8,128)(2,1)} %bitcast.9, f32[20,640]{1,0:T(8,128)} %sent_hbm.1, s32[20,640]{1,0:T(8,128)} %wet_ref.1, f32[20,640]{1,0:T(8,128)} %diff_ref.1, ...), custom_call_target="tpu_custom_call" | custom-call | tf_op jit(solution)/shard_map/pack/pallas_call | solution.py:384
  4.1 17.8 %all-to-all-start = ((bf16[32,144,128]{2,1,0:T(8,128)(2,1)}), bf16[32,144,128]{2,1,0:T(8,128)(2,1)S(1)}, u32[]{:S(2)}, u32[]{:S(2)}) async-start(bf16[32,144,128]{2,1,0:T(8,128)(2,1)} %pack.1), calls=%async_computation | async-start | bytes 2359296 | tf_op jit(solution)/shard_map/all_to_all | solution.py:418
  21.9 0.0 copy-start.1
  21.9 0.0 copy-start.2
  21.9 0.0 copy-start.3
  21.9 0.0 copy-start.4
  21.9 1.8 %rim.1 = (bf16[2,40,640]{2,1,0:T(8,128)(2,1)}, bf16[2,40,640]{2,1,0:T(8,128)(2,1)}) custom-call(s32[20,640]{1,0:T(8,128)} %wet_ref.1, f32[20,640]{1,0:T(8,128)} %diff_ref.1, bf16[20,32,640]{2,1,0:T(8,128)(2,1)} %bitcast.10), custom_call_target="tpu_custom_call" | custom-call | tf_op jit(solution)/shard_map/rim/pallas_call | solution.py:384
  23.7 0.0 copy-start
  23.7 2.1 %collective-permute-start = (bf16[2,40,640]{2,1,0:T(8,128)(2,1)}, bf16[2,40,640]{2,1,0:T(8,128)(2,1)S(1)}, u32[]{:S(2)}, u32[]{:S(2)}) collective-permute-start(bf16[2,40,640]{2,1,0:T(8,128)(2,1)} %get-tuple-element.15), channel_id=1, source_target_pairs={{0,8},{8,16},{16,24},{24,32},{32,40},{40,48},{48,56},{56,64},{64,7... | collective-permute-start | bytes 307208 | tf_op jit(solution)/shard_map/ppermute | solution.py:426
  25.8 9.3 %collective-permute-start.1 = (bf16[2,40,640]{2,1,0:T(8,128)(2,1)}, bf16[2,40,640]{2,1,0:T(8,128)(2,1)S(1)}, u32[]{:S(2)}, u32[]{:S(2)}) collective-permute-start(bf16[2,40,640]{2,1,0:T(8,128)(2,1)} %get-tuple-element.16), channel_id=1, source_target_pairs={{8,0},{16,8},{24,16},{32,24},{40,32},{48,40},{56,48},{64,56},{72,6... | collective-permute-start | bytes 307208 | tf_op jit(solution)/shard_map/ppermute | solution.py:425
  35.1 1.6 %collective-permute-done.above_ref = bf16[2,40,640]{2,1,0:T(8,128)(2,1)S(1)} collective-permute-done((bf16[2,40,640]{2,1,0:T(8,128)(2,1)}, bf16[2,40,640]{2,1,0:T(8,128)(2,1)S(1)}, u32[]{:S(2)}, u32[]{:S(2)}) %collective-permute-start) | collective-permute-done | bytes 102432 | tf_op jit(solution)/shard_map/ppermute | solution.py:426
  36.7 0.4 collective-permute-done.1.below_ref
  37.1 3.8 %all-to-all-done.recv_ref = bf16[32,144,128]{2,1,0:T(8,128)(2,1)S(1)} async-done(((bf16[32,144,128]{2,1,0:T(8,128)(2,1)}), bf16[32,144,128]{2,1,0:T(8,128)(2,1)S(1)}, u32[]{:S(2)}, u32[]{:S(2)}) %all-to-all-start) | async-done | bytes 1179680 | tf_op jit(solution)/shard_map/all_to_all | solution.py:418
  40.9 1.0 %turn.1 = bf16[256,128]{1,0:T(8,128)(2,1)} custom-call(bf16[32,144,128]{2,1,0:T(8,128)(2,1)S(1)} %all-to-all-done.recv_ref), custom_call_target="tpu_custom_call" | custom-call | tf_op jit(solution)/shard_map/turn/pallas_call | solution.py:384
  41.9 19.3 %all-to-all-start.1 = ((bf16[32,8,128]{2,1,0:T(8,128)(2,1)}), bf16[32,8,128]{2,1,0:T(8,128)(2,1)S(1)}, u32[]{:S(2)}, u32[]{:S(2)}) async-start(bf16[32,8,128]{2,1,0:T(8,128)(2,1)} %bitcast.4), calls=%async_computation.1 | async-start | bytes 131072 | tf_op jit(solution)/shard_map/all_to_all | solution.py:429
  61.2 0.0 copy-done.1
  61.2 0.0 copy-done.2
  61.2 0.0 copy-done.3
  61.2 0.0 copy-done.4
  61.2 2.1 %remap.1 = (f32[20,640]{1,0:T(8,128)}, bf16[20,32,128]{2,1,0:T(8,128)(2,1)S(1)}, f32[3,20,768]{2,1,0:T(8,128)S(1)}, bf16[2,48,128]{2,1,0:T(8,128)(2,1)S(1)}, bf16[2,48,128]{2,1,0:T(8,128)(2,1)S(1)}) custom-call(s32[3,1,8]{2,1,0:T(1,128)S(1)} %bitcast.15, bf16[32,144,128]{2,1,0:T(8,128)(2,1)S(1)} %all-to-all-done.recv_ref, bf16[8,128,128]{2,1,0:T(8,128)(2,1)S(1)} %bitcast.13, ...), custom_call_target="tpu_custom_call" | custom-call | tf_op jit(solution)/shard_map/remap/pallas_call | solution.py:384
  63.3 3.1 %collective-permute-start.2 = (bf16[2,48,128]{2,1,0:T(8,128)(2,1)S(1)}, bf16[2,48,128]{2,1,0:T(8,128)(2,1)S(1)}, u32[]{:S(2)}, u32[]{:S(2)}) collective-permute-start(bf16[2,48,128]{2,1,0:T(8,128)(2,1)S(1)} %get-tuple-element.22), channel_id=1, source_target_pairs={{0,8},{8,16},{16,24},{24,32},{32,40},{40,48},{48,56},{56,64},{64,7... | collective-permute-start | bytes 73736 | tf_op jit(solution)/shard_map/ppermute | solution.py:438
  66.4 3.7 %collective-permute-start.3 = (bf16[2,48,128]{2,1,0:T(8,128)(2,1)S(1)}, bf16[2,48,128]{2,1,0:T(8,128)(2,1)S(1)}, u32[]{:S(2)}, u32[]{:S(2)}) collective-permute-start(bf16[2,48,128]{2,1,0:T(8,128)(2,1)S(1)} %get-tuple-element.23), channel_id=1, source_target_pairs={{8,0},{16,8},{24,16},{32,24},{40,32},{48,40},{56,48},{64,56},{72,6... | collective-permute-start | bytes 73736 | tf_op jit(solution)/shard_map/ppermute | solution.py:437
  70.1 0.0 collective-permute-done.2.above2_ref
  70.1 1.4 %collective-permute-done.3.below2_ref = bf16[2,48,128]{2,1,0:T(8,128)(2,1)S(1)} collective-permute-done((bf16[2,48,128]{2,1,0:T(8,128)(2,1)S(1)}, bf16[2,48,128]{2,1,0:T(8,128)(2,1)S(1)}, u32[]{:S(2)}, u32[]{:S(2)}) %collective-permute-start.3) | collective-permute-done | bytes 24608 | tf_op jit(solution)/shard_map/ppermute | solution.py:437
  71.5 0.0 copy-done
  71.5 5.2 %step.1 = f32[20,32,640]{2,1,0:T(8,128)} custom-call(bf16[20,32,128]{2,1,0:T(8,128)(2,1)S(1)} %get-tuple-element.18.tail_ref, f32[3,20,768]{2,1,0:T(8,128)S(1)} %get-tuple-element.19.planes_ref, bf16[2,40,640]{2,1,0:T(8,128)(2,1)S(1)} %collective-permute-done.above_ref, bf16[2,40,640]{2,1,0:T(8,128)(2,1)S(1)} %collective-permute-done.1.below_ref, ...), custom_call_target="tpu_custom_call" | custom-call | tf_op jit(solution)/shard_map/step/pallas_call | solution.py:384
  76.7 0.0 all-to-all-done.1.waves_hbm
  76.7 0.0 copy-start.5
  76.7 0.6 copy-done.5
  77.3 3.3 %legendre.1 = f32[4,2,1280]{2,1,0:T(2,128)} custom-call(bf16[32,8,128]{2,1,0:T(8,128)(2,1)} %copy-done.5, bf16[1920,1280]{1,0:T(8,128)(2,1)} %bitcast.16), custom_call_target="tpu_custom_call" | custom-call | tf_op jit(solution)/shard_map/legendre/pallas_call | solution.py:384
Async XLA Ops:
  4.1 36.8 %all-to-all-start = ((bf16[32,144,128]{2,1,0:T(8,128)(2,1)}), bf16[32,144,128]{2,1,0:T(8,128)(2,1)S(1)}, u32[]{:S(2)}, u32[]{:S(2)}) async-start(bf16[32,144,128]{2,1,0:T(8,128)(2,1)} %pack.1), calls=%async_computation | async-start | bytes 2359296 | tf_op jit(solution)/shard_map/all_to_all | solution.py:418
  21.9 39.3 %copy-start.1 = (bf16[1,1,8,128,128]{4,3,2,1,0:T(8,128)(2,1)S(1)}, bf16[1,1,8,128,128]{4,3,2,1,0:T(8,128)(2,1)}, u32[]{:S(2)}) copy-start(bf16[1,1,8,128,128]{4,3,2,1,0:T(8,128)(2,1)} %param.15) | copy-start | bytes 786436
  21.9 39.3 %copy-start.2 = (s32[20,640]{1,0:T(8,128)S(1)}, s32[20,640]{1,0:T(8,128)}, u32[]{:S(2)}) copy-start(s32[20,640]{1,0:T(8,128)} %wet_ref.1) | copy-start | bytes 153604
  21.9 39.3 %copy-start.3 = (f32[20,640]{1,0:T(8,128)S(1)}, f32[20,640]{1,0:T(8,128)}, u32[]{:S(2)}) copy-start(f32[20,640]{1,0:T(8,128)} %diff_ref.1) | copy-start | bytes 153604
  21.9 39.3 %copy-start.4 = (s32[1,1,8,3]{2,1,3,0:T(1,128)S(1)}, s32[1,1,8,3]{2,1,3,0:T(1,128)}, u32[]{:S(2)}) copy-start(s32[1,1,8,3]{2,1,3,0:T(1,128)} %param.14) | copy-start | bytes 292
  23.7 47.8 %copy-start = (bf16[32,20,640]{2,0,1:T(8,128)(2,1)S(1)}, bf16[32,20,640]{2,0,1:T(8,128)(2,1)}, u32[]{:S(2)}) copy-start(bf16[32,20,640]{2,0,1:T(8,128)(2,1)} %param.9) | copy-start | bytes 2457604
  23.7 13.0 %collective-permute-start = (bf16[2,40,640]{2,1,0:T(8,128)(2,1)}, bf16[2,40,640]{2,1,0:T(8,128)(2,1)S(1)}, u32[]{:S(2)}, u32[]{:S(2)}) collective-permute-start(bf16[2,40,640]{2,1,0:T(8,128)(2,1)} %get-tuple-element.15), channel_id=1, source_target_pairs={{0,8},{8,16},{16,24},{24,32},{32,40},{40,48},{48,56},{56,64},{64,7... | collective-permute-start | bytes 307208 | tf_op jit(solution)/shard_map/ppermute | solution.py:426
  25.8 11.3 %collective-permute-start.1 = (bf16[2,40,640]{2,1,0:T(8,128)(2,1)}, bf16[2,40,640]{2,1,0:T(8,128)(2,1)S(1)}, u32[]{:S(2)}, u32[]{:S(2)}) collective-permute-start(bf16[2,40,640]{2,1,0:T(8,128)(2,1)} %get-tuple-element.16), channel_id=1, source_target_pairs={{8,0},{16,8},{24,16},{32,24},{40,32},{48,40},{56,48},{64,56},{72,6... | collective-permute-start | bytes 307208 | tf_op jit(solution)/shard_map/ppermute | solution.py:425
  41.9 34.8 %all-to-all-start.1 = ((bf16[32,8,128]{2,1,0:T(8,128)(2,1)}), bf16[32,8,128]{2,1,0:T(8,128)(2,1)S(1)}, u32[]{:S(2)}, u32[]{:S(2)}) async-start(bf16[32,8,128]{2,1,0:T(8,128)(2,1)} %bitcast.4), calls=%async_computation.1 | async-start | bytes 131072 | tf_op jit(solution)/shard_map/all_to_all | solution.py:429
  63.3 6.8 %collective-permute-start.2 = (bf16[2,48,128]{2,1,0:T(8,128)(2,1)S(1)}, bf16[2,48,128]{2,1,0:T(8,128)(2,1)S(1)}, u32[]{:S(2)}, u32[]{:S(2)}) collective-permute-start(bf16[2,48,128]{2,1,0:T(8,128)(2,1)S(1)} %get-tuple-element.22), channel_id=1, source_target_pairs={{0,8},{8,16},{16,24},{24,32},{32,40},{40,48},{48,56},{56,64},{64,7... | collective-permute-start | bytes 73736 | tf_op jit(solution)/shard_map/ppermute | solution.py:438
  66.4 5.1 %collective-permute-start.3 = (bf16[2,48,128]{2,1,0:T(8,128)(2,1)S(1)}, bf16[2,48,128]{2,1,0:T(8,128)(2,1)S(1)}, u32[]{:S(2)}, u32[]{:S(2)}) collective-permute-start(bf16[2,48,128]{2,1,0:T(8,128)(2,1)S(1)} %get-tuple-element.23), channel_id=1, source_target_pairs={{8,0},{16,8},{24,16},{32,24},{40,32},{48,40},{56,48},{64,56},{72,6... | collective-permute-start | bytes 73736 | tf_op jit(solution)/shard_map/ppermute | solution.py:437
  76.7 0.6 copy-start.5
